TPU v7x, 256 devices: a whole 4x4x8 slice. The times are simulated.
256 devices in a mesh: dp: 16 (over x, y), expert: 16 (over z, core).
Axes of the slice: x: 4, y: 4, z: 8, core: 2. Of those that a mesh axis runs over, the one named last changes fastest.
Arguments:
- tokens: bfloat16 [32768, 2048], P(('dp', 'expert')), may hold values from -70 to 70
- routing: int32 [32768, 2], P(('dp', 'expert')), may hold values from 0 to 15, all different within a row; in each aligned block of 128 rows (0 to 127, 128 to 255, ...) at most 20 rows name the same one
- probs: bfloat16 [32768, 2], P(('dp', 'expert')), may hold values from 0.099609375 to 1
- cotangent: bfloat16 [32768, 2048], P(('dp', 'expert')), may hold values from -70 to 70
- w_gate: bfloat16 [16, 2048, 512], P('expert'), may hold values from -0.125 to 0.125
- w_up: bfloat16 [16, 2048, 512], P('expert'), may hold values from -0.125 to 0.125
- w_down: bfloat16 [16, 512, 2048], P('expert'), may hold values from -0.25 to 0.25
Outputs:
- grad_gate: float32 [16, 2048, 512], P('expert', 'dp')
- grad_up: float32 [16, 2048, 512], P('expert', 'dp')
- grad_down: float32 [16, 512, 2048], P('expert', None, 'dp')
- input_grad: bfloat16 [32768, 2048], P(('dp', 'expert'))
- router_grad: bfloat16 [32768, 2], P(('dp', 'expert'))
Inputs may be any that keep to these rules, and one draw needn't show every extreme that they name: `routing`: each row names 2 different experts. Among the 128 rows of one device no expert is named more than 20 times, a bound that some block reaches.
All inputs are finite; a program needn't handle non-finite values.
Results may differ from a plain program's by a relative error of at most 0.0065.
Values may be sent and summed in bfloat16 or wider, within the bound.
No kernel may reach another device: no remote copies, remote signals or barrier semaphores. Data moves between devices by JAX's collectives and lax.ppermute only.
A program may use at most 64 MiB of HBM per device.

v0:
```python
import jax
import jax.numpy as jnp
from jax import lax
from jax.sharding import PartitionSpec as P

epsilon = 1e-06


def partner_2(value, axis, stride):
    mask = 2**stride
    pairs = [(source, source ^ mask) for source in range(lax.axis_size(axis))]
    return lax.ppermute(value, axis, pairs)


def in_one_piece(arrays, axis, split_dim, concat_dim, along):
    columns = [a.reshape(*a.shape[:along], -1) for a in arrays]
    both = jnp.concatenate(columns, axis=along)
    whole, at, done = (
        lax.all_to_all(both, axis, split_axis=split_dim, concat_axis=concat_dim, tiled=True),
        0,
        [],
    )
    for a, column in zip(arrays, columns):
        piece = whole[..., at : at + column.shape[along]]
        done.append(piece.reshape(*piece.shape[:along], *a.shape[along:]))
        at += column.shape[along]
    return tuple(done)


def contract(former, latter, former_dim, latter_dim):
    return lax.dot_general(
        former,
        latter,
        (((former_dim,), (latter_dim,)), ((), ())),
        preferred_element_type=jnp.float32,
    )


def expert_pass(routed, cot_rows, prob_rows, gate_matrix, up_matrix, down_matrix):
    gate_pre = jnp.dot(routed, gate_matrix, preferred_element_type=jnp.float32)
    up_pre = jnp.dot(routed, up_matrix, preferred_element_type=jnp.float32)
    sigmoid = jax.nn.sigmoid(gate_pre)
    activated = gate_pre * sigmoid
    hidden = (activated * up_pre).astype(jnp.bfloat16)
    output = jnp.dot(hidden, down_matrix, preferred_element_type=jnp.float32)
    router_slots = jnp.sum(output * cot_rows.astype(jnp.float32), axis=1).astype(jnp.bfloat16)
    scaled = (prob_rows.astype(jnp.float32)[:, None] * cot_rows.astype(jnp.float32)).astype(
        jnp.bfloat16
    )
    hidden_grad = contract(scaled, down_matrix, 1, 1)
    up_grad = (hidden_grad * activated).astype(jnp.bfloat16)
    gate_grad = (hidden_grad * up_pre * sigmoid * (1.0 + gate_pre * (1.0 - sigmoid))).astype(
        jnp.bfloat16
    )
    routed_grad = (
        contract(gate_grad, gate_matrix, 1, 1) + contract(up_grad, up_matrix, 1, 1)
    ).astype(jnp.bfloat16)
    return (hidden, scaled, gate_grad, up_grad, routed_grad, router_slots)


def weight_grads(routed, scaled, gate_grad, up_grad, hidden, scaling):
    return (
        jnp.stack(
            [
                contract(routed, gate_grad, 0, 0),
                contract(routed, up_grad, 0, 0),
                contract(scaled, hidden, 0, 0),
            ]
        )
        * scaling
    )


def split_halves(portion, own_bit):
    halfway = portion.shape[1] // 2
    retained = lax.dynamic_slice_in_dim(portion, own_bit * halfway, halfway, 1)
    handed = lax.dynamic_slice_in_dim(portion, (1 - own_bit) * halfway, halfway, 1)
    return (retained, handed)


def group_totals(totals, levels, which_bit):
    for higher in range(which_bit, levels):
        totals = totals + partner_2(totals, "dp", higher)
    return totals


def adasum_pair(retained, partner, own_bit, levels, which_bit):
    own_sq = jnp.sum(retained * retained, axis=(1, 2))
    partner_sq = jnp.sum(partner * partner, axis=(1, 2))
    inner_sum = jnp.sum(retained * partner, axis=(1, 2))
    is_former = own_bit == 0
    former_sq = jnp.where(is_former, own_sq, partner_sq)
    latter_sq = jnp.where(is_former, partner_sq, own_sq)
    totals = jnp.stack([former_sq, latter_sq, inner_sum])
    totals = group_totals(totals, levels, which_bit)
    former_coef = 1.0 - totals[2] / (2.0 * (totals[0] + epsilon))
    latter_coef = 1.0 - totals[2] / (2.0 * (totals[1] + epsilon))
    own_coef = jnp.where(is_former, former_coef, latter_coef)
    partner_coef = jnp.where(is_former, latter_coef, former_coef)
    return own_coef[:, None, None] * retained + partner_coef[:, None, None] * partner


def per_device(tokens, routing, probs, cotangent, w_gate, w_up, w_down):
    experts = lax.axis_size("expert")
    rows_here, top_count = routing.shape
    model_width = tokens.shape[1]
    capacity = 5 * rows_here * top_count // (4 * experts)
    choices = rows_here * top_count
    slot_total = experts * capacity
    flattened = routing.reshape(-1)
    onehot = (flattened[:, None] == jnp.arange(experts, dtype=jnp.int32)[None, :]).astype(jnp.int32)
    before = jnp.cumsum(onehot, axis=0) - onehot
    destination = flattened * capacity + jnp.sum(before * onehot, axis=1)
    source = (
        jnp.full((slot_total,), choices, jnp.int32)
        .at[destination]
        .set(jnp.arange(choices, dtype=jnp.int32))
    )
    token_of = jnp.where(source < choices, source // top_count, rows_here)
    send_rows = jnp.take(tokens, token_of, axis=0, mode="fill", fill_value=0)
    send_cot = jnp.take(cotangent, token_of, axis=0, mode="fill", fill_value=0)
    send_prob = jnp.take(probs.reshape(-1), source, axis=0, mode="fill", fill_value=0)
    routed, cot_rows, prob_rows = in_one_piece(
        (
            send_rows.reshape(experts, capacity, model_width),
            send_cot.reshape(experts, capacity, model_width),
            send_prob.reshape(experts, capacity),
        ),
        "expert",
        0,
        0,
        2,
    )
    routed = routed.reshape(slot_total, model_width)
    cot_rows = cot_rows.reshape(slot_total, model_width)
    prob_rows = prob_rows.reshape(slot_total)
    hidden, scaled, gate_grad, up_grad, routed_grad, router_slots = expert_pass(
        routed, cot_rows, prob_rows, w_gate[0], w_up[0], w_down[0]
    )
    arrived_grad, arrived_router = (
        lax.all_to_all(
            routed_grad.reshape(experts, capacity, model_width),
            "expert",
            split_axis=0,
            concat_axis=0,
            tiled=True,
        ),
        lax.all_to_all(
            router_slots.reshape(experts, capacity),
            "expert",
            split_axis=0,
            concat_axis=0,
            tiled=True,
        ),
    )
    picked = arrived_grad.reshape(slot_total, model_width)[destination]
    input_grad = jnp.sum(
        picked.reshape(rows_here, top_count, model_width).astype(jnp.float32), axis=1
    )
    input_grad = input_grad.astype(jnp.bfloat16)
    router_grad = arrived_router.reshape(slot_total)[destination].reshape(rows_here, top_count)
    scaling = 1.0 / slot_total
    levels = lax.axis_size("dp").bit_length() - 1
    position = lax.axis_index("dp")
    top_bit = position >> levels - 1 & 1
    halfway = model_width // 2
    hidden_width = hidden.shape[1]
    routed_kept = lax.dynamic_slice_in_dim(routed, top_bit * halfway, halfway, 1)
    routed_handed = lax.dynamic_slice_in_dim(routed, (1 - top_bit) * halfway, halfway, 1)
    scaled_kept = lax.dynamic_slice_in_dim(scaled, top_bit * halfway, halfway, 1)
    scaled_handed = lax.dynamic_slice_in_dim(scaled, (1 - top_bit) * halfway, halfway, 1)
    retained = weight_grads(routed_kept, scaled_kept, gate_grad, up_grad, hidden, scaling)
    bundle = jnp.concatenate([routed_handed, scaled_handed, gate_grad, up_grad, hidden], axis=1)
    received = partner_2(bundle, "dp", levels - 1)
    mark = 2 * halfway
    partner = weight_grads(
        received[:, :halfway],
        received[:, halfway:mark],
        received[:, mark : mark + hidden_width],
        received[:, mark + hidden_width : mark + 2 * hidden_width],
        received[:, mark + 2 * hidden_width :],
        scaling,
    )
    portion = adasum_pair(retained, partner, top_bit, levels, levels - 1)
    for halving in range(1, levels):
        which_bit = levels - 1 - halving
        own_bit = position >> which_bit & 1
        retained, handed = split_halves(portion, own_bit)
        partner = partner_2(handed.astype(jnp.bfloat16), "dp", which_bit).astype(handed.dtype)
        portion = adasum_pair(retained, partner, own_bit, levels, which_bit)
    return (portion[0][None], portion[1][None], portion[2].T[None], input_grad, router_grad)


def solution(mesh):
    placed = (
        P(("dp", "expert"), None),
        P(("dp", "expert"), None),
        P(("dp", "expert"), None),
        P(("dp", "expert"), None),
        P("expert", None, None),
        P("expert", None, None),
        P("expert", None, None),
    )
    return jax.shard_map(
        per_device,
        mesh=mesh,
        in_specs=placed,
        out_specs=(
            P("expert", "dp", None),
            P("expert", "dp", None),
            P("expert", None, "dp"),
            P(("dp", "expert"), None),
            P(("dp", "expert"), None),
        ),
        check_vma=False,
    )
```

profile of v0, /device:TPU:2, one launch (start us, length us, event | category | flops | bytes accessed | tf_op | source)
XLA Modules:
  0.0 344.7 jit_solution(16997646244204736950)
XLA Ops:
  8.8 3.0 gather_fusion.4
  14.9 3.0 broadcast_select_fusion.1
  17.9 3.2 reshape.452
  22.4 3.9 %pad_maximum_fusion.2 = bf16[16,20,4097]{2,1,0:T(8,128)(2,1)} fusion(bf16[16,20,1]{2,1,0:T(8,128)(2,1)S(1)} %select_n.313, bf16[16,20,2048]{2,1,0:T(8,128)(2,1)} %reshape.453, bf16[16,20,2048]{2,1,0:T(8,128)(2,1)} %reshape.452), kind=kLoop, calls=%fused_computation.15 | loop fusion | flops 7866240 | bytes 5244160 | tf_op jit(solution)/shard_map/concatenate | solution.py:17
  26.2 8.6 %all-to-all-start = ((bf16[16,20,4097]{2,1,0:T(8,128)(2,1)}), bf16[16,20,4097]{2,1,0:T(8,128)(2,1)}, u32[]{:S(2)}, u32[]{:S(2)}) async-start(bf16[16,20,4097]{2,1,0:T(8,128)(2,1)} %pad_maximum_fusion.2), calls=%async_computation | async-start | bytes 6488064 | tf_op jit(solution)/shard_map/all_to_all | solution.py:19
  34.9 74.0 %all-to-all-done = bf16[16,20,4097]{2,1,0:T(8,128)(2,1)} async-done(((bf16[16,20,4097]{2,1,0:T(8,128)(2,1)}), bf16[16,20,4097]{2,1,0:T(8,128)(2,1)}, u32[]{:S(2)}, u32[]{:S(2)}) %all-to-all-start) | async-done | bytes 2622112 | tf_op jit(solution)/shard_map/all_to_all | solution.py:19
  112.8 3.3 convert_element_type.93
  116.1 4.7 %slice_convert_fusion = (f32[16,20,2048]{2,1,0:T(8,128)}, bf16[16,20,2048]{2,1,0:T(8,128)(2,1)}) fusion(bf16[16,20,4097]{2,1,0:T(8,128)(2,1)} %all-to-all-done), kind=kLoop, calls=%fused_computation.48 | loop fusion | flops 655360 | bytes 6553600 | tf_op jit(solution)/shard_map/convert_element_type | solution.py:47
  120.8 4.1 %reshape.463 = f32[320,2048]{1,0:T(8,128)} reshape(f32[16,20,2048]{2,1,0:T(8,128)} %get-tuple-element.53) | data formatting | bytes 5242880 | tf_op jit(solution)/shard_map/convert_element_type | solution.py:47
  143.6 47.4 %collective-permute-done = bf16[320,3584]{1,0:T(8,128)(2,1)} collective-permute-done((bf16[320,3584]{1,0:T(8,128)(2,1)}, bf16[320,3584]{1,0:T(8,128)(2,1)}, u32[]{:S(2)}, u32[]{:S(2)}) %collective-permute-start) | collective-permute-done | bytes 2293792 | tf_op jit(solution)/shard_map/ppermute | solution.py:12
  211.4 3.3 fusion.17
  215.5 5.1 %all-to-all-start.2 = ((bf16[16,1,20]{2,1,0:T(2,128)(2,1)}), bf16[16,1,20]{2,1,0:T(2,128)(2,1)S(1)}, u32[]{:S(2)}, u32[]{:S(2)}) async-start(bf16[16,1,20]{2,1,0:T(2,128)(2,1)} %convert_element_type.114), calls=%async_computation.2 | async-start | bytes 16384 | tf_op jit(solution)/shard_map/all_to_all | solution.py:148
  220.5 24.6 %collective-permute-done.2 = bf16[3,512,512]{2,1,0:T(8,128)(2,1)} collective-permute-done((bf16[3,512,512]{2,1,0:T(8,128)(2,1)}, bf16[3,512,512]{2,1,0:T(8,128)(2,1)}, u32[]{:S(2)}, u32[]{:S(2)}) %collective-permute-start.2) | collective-permute-done | bytes 1572896 | tf_op jit(solution)/shard_map/ppermute | solution.py:12
  245.1 3.4 multiply_reduce_fusion.3
  249.2 3.0 collective-permute-done.3
  262.4 3.2 collective-permute-start.5
  268.7 5.7 %all-to-all-start.1 = ((bf16[16,20,2048]{2,1,0:T(8,128)(2,1)}), bf16[16,20,2048]{2,1,0:T(8,128)(2,1)}, u32[]{:S(2)}, u32[]{:S(2)}) async-start(bf16[16,20,2048]{2,1,0:T(8,128)(2,1)} %reshape.456), calls=%async_computation.1 | async-start | bytes 3145728 | tf_op jit(solution)/shard_map/all_to_all | solution.py:141
  274.4 3.6 %collective-permute-done.5 = bf16[3,256,512]{2,1,0:T(8,128)(2,1)} collective-permute-done((bf16[3,256,512]{2,1,0:T(8,128)(2,1)}, bf16[3,256,512]{2,1,0:T(8,128)(2,1)}, u32[]{:S(2)}, u32[]{:S(2)}) %collective-permute-start.5) | collective-permute-done | bytes 786464 | tf_op jit(solution)/shard_map/ppermute | solution.py:12
  280.2 3.3 collective-permute-start.6
  286.0 3.0 collective-permute-done.7
  302.7 9.6 %all-to-all-done.1 = bf16[16,20,2048]{2,1,0:T(8,128)(2,1)} async-done(((bf16[16,20,2048]{2,1,0:T(8,128)(2,1)}), bf16[16,20,2048]{2,1,0:T(8,128)(2,1)}, u32[]{:S(2)}, u32[]{:S(2)}) %all-to-all-start.1) | async-done | bytes 1310752 | tf_op jit(solution)/shard_map/all_to_all | solution.py:141
  318.6 3.6 %reduce_sum.154 = bf16[128,2048]{1,0:T(8,128)(2,1)} reduce(bf16[128,2,2048]{2,1,0:T(2,128)(2,1)S(1)} %reshape.458, bf16[]{:T(256)} %constant.71.clone.1), dimensions={1}, to_apply=%region_16.18 | reduce | flops 262144 | bytes 1572866 | tf_op jit(solution)/shard_map/reduce_sum | solution.py:157
  328.4 4.3 %collective-permute-done.11 = f32[3,3]{1,0:T(4,128)S(1)} collective-permute-done((f32[3,3]{1,0:T(4,128)S(1)}, f32[3,3]{1,0:T(4,128)S(1)}, u32[]{:S(2)}, u32[]{:S(2)}) %collective-permute-start.11) | collective-permute-done | bytes 68 | tf_op jit(solution)/shard_map/ppermute | solution.py:12
  333.3 3.0 collective-permute-done.12
  (146 shorter events, 109.5 us)
Async XLA Ops:
  0.6 133.1 %copy-start = (bf16[1,2048,512]{2,1,0:T(8,128)(2,1)S(1)}, bf16[1,2048,512]{2,1,0:T(8,128)(2,1)}, u32[]{:S(2)}) copy-start(bf16[1,2048,512]{2,1,0:T(8,128)(2,1)} %param.13) | copy-start | bytes 6291460
  0.6 8.1 %copy-start.1 = (bf16[128,2048]{1,0:T(8,128)(2,1)S(1)}, bf16[128,2048]{1,0:T(8,128)(2,1)}, u32[]{:S(2)}) copy-start(bf16[128,2048]{1,0:T(8,128)(2,1)} %param.12) | copy-start | bytes 1572868
  26.2 82.6 %all-to-all-start = ((bf16[16,20,4097]{2,1,0:T(8,128)(2,1)}), bf16[16,20,4097]{2,1,0:T(8,128)(2,1)}, u32[]{:S(2)}, u32[]{:S(2)}) async-start(bf16[16,20,4097]{2,1,0:T(8,128)(2,1)} %pad_maximum_fusion.2), calls=%async_computation | async-start | bytes 6488064 | tf_op jit(solution)/shard_map/all_to_all | solution.py:19
  127.3 3.5 %copy-start.14 = (bf16[1,512,2048]{2,1,0:T(8,128)(2,1)S(1)}, bf16[1,512,2048]{2,1,0:T(8,128)(2,1)}, u32[]{:S(2)}) copy-start(bf16[1,512,2048]{2,1,0:T(8,128)(2,1)} %param.15) | copy-start | bytes 6291460
  127.3 3.5 %copy-start.15 = (bf16[320,2048]{1,0:T(8,128)(2,1)S(1)}, bf16[320,2048]{1,0:T(8,128)(2,1)}, u32[]{:S(2)}) copy-start(bf16[320,2048]{1,0:T(8,128)(2,1)} %convert_element_type.93) | copy-start | bytes 3932164
  137.8 53.2 %collective-permute-start = (bf16[320,3584]{1,0:T(8,128)(2,1)}, bf16[320,3584]{1,0:T(8,128)(2,1)}, u32[]{:S(2)}, u32[]{:S(2)}) collective-permute-start(bf16[320,3584]{1,0:T(8,128)(2,1)} %get-tuple-element.45), channel_id=1, source_target_pairs={{0,128},{16,144},{32,160},{48,176},{64,192},{80,208},{96,224},{112... | collective-permute-start | bytes 6881288 | tf_op jit(solution)/shard_map/ppermute | solution.py:12
  199.5 5.2 %collective-permute-start.1 = (f32[3,3]{1,0:T(4,128)S(1)}, f32[3,3]{1,0:T(4,128)S(1)}, u32[]{:S(2)}, u32[]{:S(2)}) collective-permute-start(f32[3,3]{1,0:T(4,128)S(1)} %pad_maximum_fusion.3), channel_id=1, source_target_pairs={{0,128},{16,144},{32,160},{48,176},{64,192},{80,208},{96,224},{112... | collective-permute-start | bytes 116 | tf_op jit(solution)/shard_map/ppermute | solution.py:12
  210.9 34.2 %collective-permute-start.2 = (bf16[3,512,512]{2,1,0:T(8,128)(2,1)}, bf16[3,512,512]{2,1,0:T(8,128)(2,1)}, u32[]{:S(2)}, u32[]{:S(2)}) collective-permute-start(bf16[3,512,512]{2,1,0:T(8,128)(2,1)} %dynamic-slice_convert_fusion), channel_id=1, source_target_pairs={{0,64},{16,80},{32,96},{48,112},{64,0},{80,16},{96,32},{112,48},{1... | collective-permute-start | bytes 4718600 | tf_op jit(solution)/shard_map/ppermute | solution.py:12
  215.5 53.2 %all-to-all-start.2 = ((bf16[16,1,20]{2,1,0:T(2,128)(2,1)}), bf16[16,1,20]{2,1,0:T(2,128)(2,1)S(1)}, u32[]{:S(2)}, u32[]{:S(2)}) async-start(bf16[16,1,20]{2,1,0:T(2,128)(2,1)} %convert_element_type.114), calls=%async_computation.2 | async-start | bytes 16384 | tf_op jit(solution)/shard_map/all_to_all | solution.py:148
  248.5 3.7 %collective-permute-start.3 = (f32[3,3]{1,0:T(4,128)S(1)}, f32[3,3]{1,0:T(4,128)S(1)}, u32[]{:S(2)}, u32[]{:S(2)}) collective-permute-start(f32[3,3]{1,0:T(4,128)S(1)} %pad_maximum_fusion.4), channel_id=1, source_target_pairs={{0,64},{16,80},{32,96},{48,112},{64,0},{80,16},{96,32},{112,48},{1... | collective-permute-start | bytes 116 | tf_op jit(solution)/shard_map/ppermute | solution.py:12
  252.2 5.2 %collective-permute-start.4 = (f32[3,3]{1,0:T(4,128)S(1)}, f32[3,3]{1,0:T(4,128)S(1)}, u32[]{:S(2)}, u32[]{:S(2)}) collective-permute-start(f32[3,3]{1,0:T(4,128)S(1)} %fusion.73), channel_id=1, source_target_pairs={{0,128},{16,144},{32,160},{48,176},{64,192},{80,208},{96,224},{112... | collective-permute-start | bytes 116 | tf_op jit(solution)/shard_map/ppermute | solution.py:12
  257.4 8.1 %copy-start.12 = (bf16[320,512]{1,0:T(8,128)(2,1)S(1)}, bf16[320,512]{1,0:T(8,128)(2,1)}, u32[]{:S(2)}) copy-start(bf16[320,512]{1,0:T(8,128)(2,1)} %get-tuple-element.50) | copy-start | bytes 983044
  262.4 4.1 %copy-start.10 = (bf16[320,512]{1,0:T(8,128)(2,1)S(1)}, bf16[320,512]{1,0:T(8,128)(2,1)}, u32[]{:S(2)}) copy-start(bf16[320,512]{1,0:T(8,128)(2,1)} %get-tuple-element.48) | copy-start | bytes 983044
  262.4 4.1 %copy-start.13 = (bf16[1,2048,512]{2,1,0:T(8,128)(2,1)S(1)}, bf16[1,2048,512]{2,1,0:T(8,128)(2,1)}, u32[]{:S(2)}) copy-start(bf16[1,2048,512]{2,1,0:T(8,128)(2,1)} %param.14) | copy-start | bytes 6291460
  262.4 15.6 %collective-permute-start.5 = (bf16[3,256,512]{2,1,0:T(8,128)(2,1)}, bf16[3,256,512]{2,1,0:T(8,128)(2,1)}, u32[]{:S(2)}, u32[]{:S(2)}) collective-permute-start(bf16[3,256,512]{2,1,0:T(8,128)(2,1)} %dynamic-slice_convert_fusion.1), channel_id=1, source_target_pairs={{0,32},{16,48},{32,0},{48,16},{64,96},{80,112},{96,64},{112,80},{1... | collective-permute-start | bytes 2359304 | tf_op jit(solution)/shard_map/ppermute | solution.py:12
  268.7 43.6 %all-to-all-start.1 = ((bf16[16,20,2048]{2,1,0:T(8,128)(2,1)}), bf16[16,20,2048]{2,1,0:T(8,128)(2,1)}, u32[]{:S(2)}, u32[]{:S(2)}) async-start(bf16[16,20,2048]{2,1,0:T(8,128)(2,1)} %reshape.456), calls=%async_computation.1 | async-start | bytes 3145728 | tf_op jit(solution)/shard_map/all_to_all | solution.py:141
  280.2 5.2 %collective-permute-start.6 = (f32[3,3]{1,0:T(4,128)S(1)}, f32[3,3]{1,0:T(4,128)S(1)}, u32[]{:S(2)}, u32[]{:S(2)}) collective-permute-start(f32[3,3]{1,0:T(4,128)S(1)} %pad_maximum_fusion.5), channel_id=1, source_target_pairs={{0,32},{16,48},{32,0},{48,16},{64,96},{80,112},{96,64},{112,80},{1... | collective-permute-start | bytes 116 | tf_op jit(solution)/shard_map/ppermute | solution.py:12
  285.4 3.7 %collective-permute-start.7 = (f32[3,3]{1,0:T(4,128)S(1)}, f32[3,3]{1,0:T(4,128)S(1)}, u32[]{:S(2)}, u32[]{:S(2)}) collective-permute-start(f32[3,3]{1,0:T(4,128)S(1)} %fusion.72), channel_id=1, source_target_pairs={{0,64},{16,80},{32,96},{48,112},{64,0},{80,16},{96,32},{112,48},{1... | collective-permute-start | bytes 116 | tf_op jit(solution)/shard_map/ppermute | solution.py:12
  289.1 5.2 %collective-permute-start.8 = (f32[3,3]{1,0:T(4,128)S(1)}, f32[3,3]{1,0:T(4,128)S(1)}, u32[]{:S(2)}, u32[]{:S(2)}) collective-permute-start(f32[3,3]{1,0:T(4,128)S(1)} %fusion.93), channel_id=1, source_target_pairs={{0,128},{16,144},{32,160},{48,176},{64,192},{80,208},{96,224},{112... | collective-permute-start | bytes 116 | tf_op jit(solution)/shard_map/ppermute | solution.py:12
  298.2 24.0 %collective-permute-start.9 = (bf16[3,128,512]{2,1,0:T(8,128)(2,1)}, bf16[3,128,512]{2,1,0:T(8,128)(2,1)}, u32[]{:S(2)}, u32[]{:S(2)}) collective-permute-start(bf16[3,128,512]{2,1,0:T(8,128)(2,1)} %dynamic-slice_convert_fusion.2), channel_id=1, source_target_pairs={{0,16},{16,0},{32,48},{48,32},{64,80},{80,64},{96,112},{112,96},{1... | collective-permute-start | bytes 1179656 | tf_op jit(solution)/shard_map/ppermute | solution.py:12
  323.8 3.7 %collective-permute-start.10 = (f32[3,3]{1,0:T(4,128)S(1)}, f32[3,3]{1,0:T(4,128)S(1)}, u32[]{:S(2)}, u32[]{:S(2)}) collective-permute-start(f32[3,3]{1,0:T(4,128)S(1)} %pad_maximum_fusion.6), channel_id=1, source_target_pairs={{0,16},{16,0},{32,48},{48,32},{64,80},{80,64},{96,112},{112,96},{1... | collective-permute-start | bytes 116 | tf_op jit(solution)/shard_map/ppermute | solution.py:12
  327.5 5.2 %collective-permute-start.11 = (f32[3,3]{1,0:T(4,128)S(1)}, f32[3,3]{1,0:T(4,128)S(1)}, u32[]{:S(2)}, u32[]{:S(2)}) collective-permute-start(f32[3,3]{1,0:T(4,128)S(1)} %fusion.71), channel_id=1, source_target_pairs={{0,32},{16,48},{32,0},{48,16},{64,96},{80,112},{96,64},{112,80},{1... | collective-permute-start | bytes 116 | tf_op jit(solution)/shard_map/ppermute | solution.py:12
  332.7 3.7 %collective-permute-start.12 = (f32[3,3]{1,0:T(4,128)S(1)}, f32[3,3]{1,0:T(4,128)S(1)}, u32[]{:S(2)}, u32[]{:S(2)}) collective-permute-start(f32[3,3]{1,0:T(4,128)S(1)} %fusion.92), channel_id=1, source_target_pairs={{0,64},{16,80},{32,96},{48,112},{64,0},{80,16},{96,32},{112,48},{1... | collective-permute-start | bytes 116 | tf_op jit(solution)/shard_map/ppermute | solution.py:12
  336.4 5.1 %collective-permute-start.13 = (f32[3,3]{1,0:T(4,128)S(1)}, f32[3,3]{1,0:T(4,128)S(1)}, u32[]{:S(2)}, u32[]{:S(2)}) collective-permute-start(f32[3,3]{1,0:T(4,128)S(1)} %add.230), channel_id=1, source_target_pairs={{0,128},{16,144},{32,160},{48,176},{64,192},{80,208},{96,224},{112... | collective-permute-start | bytes 116 | tf_op jit(solution)/shard_map/ppermute | solution.py:12
  (9 other events, 18.2 us)
where the time goes:
time: 346 us; the launch traced here: 345 us
  waiting for transfers between devices  189 us (55%)
  local copies, waits for them, and re-layouts  50.4 us (15%)
  starting transfers between devices  42.4 us (12%)
  other arithmetic  41.9 us (12%)
  matrix products  19.7 us (6%)
    ppermute x14, waiting for transfers between devices, partner_2(): return lax.ppermute(value, axis, pairs)  106 us
    all_to_all x1, waiting for transfers between devices, in_one_piece(): lax.all_to_all(both, axis, split_axis=split_dim, concat_axis=concat_dim,...  74 us
    ppermute x14, starting transfers between devices, partner_2(): return lax.ppermute(value, axis, pairs)  23 us
    dot_general x9, matrix products, contract(): lax.dot_general(former, latter, (((former_dim,), (latter_dim,)), ((), ())...  11.9 us
    unnamed x38, local copies, waits for them, and re-layouts  10.6 us
    reduce_sum x4, other arithmetic, adasum_pair(): own_sq = jnp.sum(retained * retained, axis=(1, 2))  9.89 us
    all_to_all x1, waiting for transfers between devices, per_device(): lax.all_to_all(routed_grad.reshape(experts, capacity, model_width), 'expe...  9.61 us
    add x4, other arithmetic, adasum_pair(): own_coef[:, None, None] * retained + partner_coef[:, None, None] * partner  8.62 us
  transfers between devices with their start and end apart: 17, of which 15 were waited for; matrix products, arithmetic and copies ran while one was open for 10% of the time, Pallas kernels for 0%

commit v1 on v0

v1 whole, which is shorter than its diff:
```python
import functools

import jax
import jax.numpy as jnp
from jax import lax
from jax.experimental import pallas as pl
from jax.experimental.pallas import tpu as pltpu
from jax.sharding import PartitionSpec as P

epsilon = 1e-06
VMEM = pl.BlockSpec(memory_space=pltpu.VMEM)
F32 = jnp.float32
BF16 = jnp.bfloat16


def params(mib):
    return pltpu.CompilerParams(vmem_limit_bytes=mib << 20)


def iota(shape, dim):
    return lax.broadcasted_iota(jnp.int32, shape, dim)


def quotient(value, divisor, limit):
    factor = -(-(1 << 20) // divisor)
    assert all((v * factor) >> 20 == v // divisor for v in range(limit))
    return (value * factor) >> 20


def flag(condition):
    return jnp.where(condition, 1.0, 0.0)


def matmul(a, b, a_dim=1, b_dim=0, precision=None):
    return lax.dot_general(
        a, b, (((a_dim,), (b_dim,)), ((), ())), precision=precision, preferred_element_type=F32
    )


def occupants(routing_rows, expert_of, slot_of, tokens):
    first = flag(routing_rows[0:1, :] == expert_of)
    second = flag(routing_rows[1:2, :] == expert_of)
    named = first + second
    shape = (tokens, tokens)
    earlier = flag(iota(shape, 0) < iota(shape, 1)).astype(BF16)
    count = matmul(named.astype(BF16), earlier)
    taken = named * flag(count == slot_of.astype(F32))
    return taken, first, second


def dispatch_kernel(experts, capacity, routing_ref, probs_ref, tokens_ref, cot_ref, out_ref):
    tokens, width = tokens_ref.shape
    rows = out_ref.shape[0]
    row = iota((rows, tokens), 0)
    expert_of = quotient(row, 2 * capacity, rows)
    place = row - expert_of * (2 * capacity)
    is_cot = flag(place >= capacity)
    slot_of = jnp.where(place >= capacity, place - capacity, place)
    taken, first, second = occupants(routing_ref[...], expert_of, slot_of, tokens)
    probs = probs_ref[...].astype(F32)
    weight = first * probs[0:1, :] + second * probs[1:2, :]
    pick = jnp.concatenate(
        [(taken * (1.0 - is_cot)).astype(BF16), (taken * is_cot * weight).astype(BF16)], axis=1
    )
    step = 512
    for at in range(0, width, step):
        both = jnp.concatenate([tokens_ref[:, at : at + step], cot_ref[:, at : at + step]], axis=0)
        out_ref[:, at : at + step] = matmul(pick, both).astype(BF16)


def expert_kernel(
    experts, capacity, mixed_ref, gate_ref, up_ref, down_ref,
    blocks_ref, gate_grad_ref, up_grad_ref, router_ref, routed_ref, scaled_ref,
):
    slots, width = routed_ref.shape
    hidden_width = gate_ref.shape[1]
    rows = mixed_ref.shape[0]
    slot = iota((slots, rows), 0)
    source = slot + quotient(slot, capacity, slots) * capacity
    column = iota((slots, rows), 1)
    pick_routed = flag(column == source).astype(BF16)
    pick_scaled = flag(column == source + capacity).astype(BF16)
    step = 512
    for at in range(0, width, step):
        part = mixed_ref[:, at : at + step]
        routed_ref[:, at : at + step] = matmul(pick_routed, part).astype(BF16)
        scaled_ref[:, at : at + step] = matmul(pick_scaled, part).astype(BF16)
    routed = routed_ref[...]
    scaled = scaled_ref[...]
    gate_pre = matmul(routed, gate_ref[...])
    up_pre = matmul(routed, up_ref[...])
    hidden_grad = matmul(scaled, down_ref[...], 1, 1)
    sigmoid = 1.0 / (1.0 + jnp.exp(-gate_pre))
    activated = gate_pre * sigmoid
    hidden = (activated * up_pre).astype(BF16)
    up_grad = (hidden_grad * activated).astype(BF16)
    gate_grad = (hidden_grad * up_pre * sigmoid * (1.0 + gate_pre * (1.0 - sigmoid))).astype(BF16)
    gate_grad_ref[...] = gate_grad
    up_grad_ref[...] = up_grad
    dots = jnp.sum(hidden.astype(F32) * hidden_grad, axis=1, keepdims=True)
    router_ref[...] = jnp.broadcast_to(dots, router_ref.shape)
    shard = blocks_ref.shape[2]
    scaling = 1.0 / slots
    step = 4 * shard
    for m, (left, right_ref) in enumerate(
        ((gate_grad, routed_ref), (up_grad, routed_ref), (hidden, scaled_ref))
    ):
        left_t = left.T
        for at in range(0, width, step):
            grads = (matmul(left_t, right_ref[:, at : at + step]) * scaling).astype(BF16)
            for j in range(step // shard):
                blocks_ref[at // shard + j, m * hidden_width : (m + 1) * hidden_width, :] = grads[
                    :, j * shard : (j + 1) * shard
                ]


def return_kernel(experts, capacity, padded, gate_grad_ref, up_grad_ref, router_ref, gate_ref, up_ref, out_ref):
    slots = gate_grad_ref.shape[0]
    width = out_ref.shape[1]
    rows = out_ref.shape[0]
    lanes = router_ref.shape[1]
    row = iota((rows, slots), 0)
    block = quotient(row, padded, rows)
    place = row - block * padded
    slot = iota((rows, slots), 1)
    slot_block = quotient(slot, capacity, slots)
    spread = (flag(slot == block * capacity + place) * flag(place < capacity)).astype(BF16)
    same = flag(slot_block == block)
    high_rows = (same * flag(place == capacity)).astype(BF16)
    low_rows = (same * flag(place == capacity + 1)).astype(BF16)
    dots = router_ref[...]
    lane_slot = iota((slots, lanes), 0)
    own_lane = flag(
        iota((slots, lanes), 1) == lane_slot - quotient(lane_slot, capacity, slots) * capacity
    )
    high = dots.astype(BF16)
    low = (dots - high.astype(F32)).astype(BF16)
    own = own_lane.astype(BF16)
    extra = matmul(high_rows, high * own) + matmul(low_rows, low * own)
    gate_grad = gate_grad_ref[...]
    up_grad = up_grad_ref[...]
    step = 512
    for at in range(0, width, step):
        rows_grad = matmul(gate_grad, gate_ref[at : at + step, :], 1, 1) + matmul(
            up_grad, up_ref[at : at + step, :], 1, 1
        )
        spread_out = matmul(spread, rows_grad.astype(BF16))
        if at == 0:
            out_ref[:, lanes:step] = spread_out[:, lanes:].astype(BF16)
            out_ref[:, 0:lanes] = (spread_out[:, :lanes] + extra).astype(BF16)
        else:
            out_ref[:, at : at + step] = spread_out.astype(BF16)


def gather_back_kernel(experts, capacity, padded, routing_ref, probs_ref, arrived_ref, grad_ref, router_ref):
    tokens, width = grad_ref.shape
    rows = arrived_ref.shape[0]
    row = iota((rows, tokens), 0)
    expert_of = quotient(row, padded, rows)
    slot_of = row - expert_of * padded
    taken, first, second = occupants(routing_ref[...], expert_of, slot_of, tokens)
    taken = taken * flag(slot_of < capacity)
    pick = taken.T.astype(BF16)
    step = 512
    for at in range(0, width, step):
        grad_ref[:, at : at + step] = matmul(pick, arrived_ref[:, at : at + step]).astype(BF16)
    lanes = tokens
    square_row = iota((rows, rows), 0)
    square_col = iota((rows, rows), 1)
    block = quotient(square_row, padded, rows)
    from_block = quotient(square_col, padded, rows)
    from_place = square_col - from_block * padded
    fetch = flag(block == from_block) * (
        flag(from_place == capacity) + flag(from_place == capacity + 1)
    )
    spread = matmul(fetch.astype(BF16), arrived_ref[:, 0:lanes])
    lane = iota((rows, lanes), 1)
    dots = jnp.sum(spread * flag(lane == slot_of), axis=1, keepdims=True)
    probs = probs_ref[...].astype(F32)
    chosen = [
        jnp.sum(taken * which * dots, axis=0, keepdims=True) for which in (first, second)
    ]
    router_ref[...] = (jnp.concatenate(chosen, axis=0) / probs).astype(BF16)


def gram_kernel(replicas, arrived_ref, out_ref):
    kinds = 3
    hidden_width = arrived_ref.shape[1] // kinds
    lanes = arrived_ref.shape[2]
    group = 16
    rows = replicas * group
    square = (rows, rows)
    same = flag((iota(square, 0) & (group - 1)) == (iota(square, 1) & (group - 1)))
    member = flag((iota((rows, lanes), 0) >> 4) == iota((rows, lanes), 1))
    fold = flag((iota((replicas, rows), 1) >> 4) == iota((replicas, rows), 0))
    result = jnp.zeros((replicas, lanes), F32)
    for m in range(kinds):
        total = jnp.zeros(square, F32)
        for at in range(m * hidden_width, (m + 1) * hidden_width, 2 * group):
            left = arrived_ref[:, at : at + group, :].reshape(rows, lanes)
            right = arrived_ref[:, at + group : at + 2 * group, :].reshape(rows, lanes)
            both = jnp.concatenate([left, right], axis=1)
            total = total + matmul(both, both, 1, 1)
        folded = matmul(total * same, member, precision=lax.Precision.HIGHEST)
        gram = matmul(fold, folded, precision=lax.Precision.HIGHEST)
        result = result + (pltpu.roll(gram, m * replicas, 1) if m else gram)
    for j in range(out_ref.shape[0]):
        out_ref[j] = result


def combine_kernel(replicas, partial_ref, arrived_ref, gate_ref, up_ref, down_ref):
    kinds = 3
    lanes = partial_ref.shape[2]
    hidden_width = arrived_ref.shape[1] // kinds
    summed = partial_ref[0]
    for j in range(1, partial_ref.shape[0]):
        summed = summed + partial_ref[j]
    row = iota((replicas, lanes), 0)
    lane = iota((replicas, lanes), 1)
    diagonal = flag(row == lane)
    inside = flag(lane < replicas)
    for m in range(kinds):
        gram = (pltpu.roll(summed, lanes - m * replicas, 1) if m else summed) * inside
        weights = diagonal
        half = replicas // 2
        while half >= 1:
            across = pltpu.roll(gram, lanes - half, 1)
            below = pltpu.roll(gram, replicas - half, 0)
            corner = pltpu.roll(across, replicas - half, 0)
            coefs = []
            for axis in (0, 1):
                former_sq = jnp.sum(gram * diagonal, axis=axis, keepdims=True)
                latter_sq = jnp.sum(corner * diagonal, axis=axis, keepdims=True)
                inner_sum = jnp.sum(across * diagonal, axis=axis, keepdims=True)
                former_sq = jnp.maximum(former_sq, 0.0)
                latter_sq = jnp.maximum(latter_sq, 0.0)
                coefs.append(
                    (
                        1.0 - inner_sum / (2.0 * (former_sq + epsilon)),
                        1.0 - inner_sum / (2.0 * (latter_sq + epsilon)),
                    )
                )
            (former_row, latter_row), (former_col, latter_col) = coefs
            live = flag(row < half) * flag(lane < half)
            gram = live * (
                former_col * (gram * former_row + across * latter_row)
                + latter_col * (below * former_row + corner * latter_row)
            )
            weights = flag(row < half) * (
                former_col * weights + latter_col * pltpu.roll(weights, replicas - half, 0)
            )
            half //= 2
        scalars = [
            jnp.sum(weights * flag(lane == d), axis=(0, 1), keepdims=True) for d in range(replicas)
        ]
        step = 128
        for at in range(0, hidden_width, step):
            start = m * hidden_width + at
            total = scalars[0] * arrived_ref[0, start : start + step, :].astype(F32)
            for d in range(1, replicas):
                total = total + scalars[d] * arrived_ref[d, start : start + step, :].astype(F32)
            if m == 2:
                down_ref[at : at + step, :] = total
            else:
                (gate_ref, up_ref)[m][:, at : at + step] = total.T


def call(kernel, name, out_shapes, mib, scratch=()):
    return pl.pallas_call(
        kernel,
        name=name,
        out_shape=out_shapes,
        scratch_shapes=scratch,
        compiler_params=params(mib),
    )


def per_device(tokens, routing, probs, cotangent, w_gate, w_up, w_down):
    experts = lax.axis_size("expert")
    replicas = lax.axis_size("dp")
    rows_here, top_count = routing.shape
    width = tokens.shape[1]
    hidden_width = w_gate.shape[2]
    capacity = 5 * rows_here * top_count // (4 * experts)
    slots = experts * capacity
    padded = capacity + 4
    shard = width // replicas
    shape = jax.ShapeDtypeStruct
    routing_rows = routing.T
    prob_rows = probs.T
    gate, up, down = w_gate[0], w_up[0], w_down[0]

    send = call(
        functools.partial(dispatch_kernel, experts, capacity),
        "dispatch", shape((2 * slots, width), BF16), 32,
    )(routing_rows, prob_rows, tokens, cotangent)
    mixed = lax.all_to_all(
        send.reshape(experts, 2 * capacity, width), "expert", 0, 0, tiled=True
    ).reshape(2 * slots, width)
    blocks, gate_grad, up_grad, router = call(
        functools.partial(expert_kernel, experts, capacity),
        "expert",
        (
            shape((replicas, 3 * hidden_width, shard), BF16),
            shape((slots, hidden_width), BF16),
            shape((slots, hidden_width), BF16),
            shape((slots, 128), F32),
        ),
        56,
        (pltpu.VMEM((slots, width), BF16), pltpu.VMEM((slots, width), BF16)),
    )(mixed, gate, up, down)
    arrived = lax.all_to_all(blocks, "dp", 0, 0, tiled=True)
    back = call(
        functools.partial(return_kernel, experts, capacity, padded),
        "return_rows", shape((experts * padded, width), BF16), 40,
    )(gate_grad, up_grad, router, gate, up)
    came_back = lax.all_to_all(
        back.reshape(experts, padded, width), "expert", 0, 0, tiled=True
    ).reshape(experts * padded, width)
    input_grad, router_grad = call(
        functools.partial(gather_back_kernel, experts, capacity, padded),
        "gather_back",
        (shape((rows_here, width), BF16), shape((top_count, rows_here), BF16)),
        32,
    )(routing_rows, prob_rows, came_back)
    partial = call(
        functools.partial(gram_kernel, replicas),
        "gram", shape((replicas, replicas, 128), F32), 40,
    )(arrived)
    partials = lax.all_to_all(partial, "dp", 0, 0, tiled=True)
    grad_gate, grad_up, grad_down = call(
        functools.partial(combine_kernel, replicas),
        "combine",
        (
            shape((shard, hidden_width), F32),
            shape((shard, hidden_width), F32),
            shape((hidden_width, shard), F32),
        ),
        40,
    )(partials, arrived)
    return (grad_gate[None], grad_up[None], grad_down[None], input_grad, router_grad.T)


def solution(mesh):
    placed = (
        P(("dp", "expert"), None),
        P(("dp", "expert"), None),
        P(("dp", "expert"), None),
        P(("dp", "expert"), None),
        P("expert", None, None),
        P("expert", None, None),
        P("expert", None, None),
    )
    return jax.shard_map(
        per_device,
        mesh=mesh,
        in_specs=placed,
        out_specs=(
            P("expert", "dp", None),
            P("expert", "dp", None),
            P("expert", None, "dp"),
            P(("dp", "expert"), None),
            P(("dp", "expert"), None),
        ),
        check_vma=False,
    )
```

time: 346 us -> 271 us (0.78)
  waiting for transfers between devices: 189 us -> 110 us
  blocking collectives: 0 us -> 69.4 us
  local copies, waits for them, and re-layouts: 50.4 us -> 6.2 us
  other arithmetic: 41.9 us -> 0 us
  Pallas kernels: 0 us -> 33.7 us
  matrix products: 19.7 us -> 0 us
  starting transfers between devices: 42.4 us -> 48.8 us
    ppermute x14 -> x0, waiting for transfers between devices: 106 us -> none  [partner_2(): return lax.ppermute(value, axis, pairs)]
    all_to_all x0 -> x1, blocking collectives: none -> 69.4 us  [per_device(): lax.all_to_all(send.reshape(experts, 2 * capacity, width), 'expert', 0, 0...]
    pallas_call x0 -> x6, Pallas kernels: none -> 33.7 us  [the longest x1 14 us: per_device(): call(functools.partial(expert_kernel, experts, capacity), 'expert', (shap...]
    all_to_all x3, starting transfers between devices: 19.4 us -> 48.8 us  [the longest x1 37.1 us: per_device(): partials = lax.all_to_all(partial, 'dp', 0, 0, tiled=True)]
    all_to_all x3, waiting for transfers between devices: 83.6 us -> 110 us  [the longest x1 75.3 us: per_device(): arrived = lax.all_to_all(blocks, 'dp', 0, 0, tiled=True)]
    ppermute x14 -> x0, starting transfers between devices: 23 us -> none  [partner_2(): return lax.ppermute(value, axis, pairs)]
    dot_general x12 -> x0, matrix products: 19.7 us -> none  [the longest x9 11.9 us: contract(): lax.dot_general(former, latter, (((former_dim,), (latter_dim,)), ((), ())...]
    reduce_sum x6 -> x0, other arithmetic: 13.6 us -> none  [the longest x4 9.89 us: adasum_pair(): own_sq = jnp.sum(retained * retained, axis=(1, 2))]
  transfers between devices with their start and end apart: 17 -> 3, of which waited for: 15 -> 3; matrix products, arithmetic and copies ran while one was open for 10% -> 0% of each run, Pallas kernels for 0% -> 5%
where the time goes in v1:
time: 271 us; the launch traced here: 269 us
  waiting for transfers between devices  110 us (41%)
  blocking collectives  69.4 us (26%)
  starting transfers between devices  48.8 us (18%)
  Pallas kernels  33.7 us (12%)
  local copies, waits for them, and re-layouts  6.2 us (2%)
    all_to_all x1, waiting for transfers between devices, per_device(): arrived = lax.all_to_all(blocks, 'dp', 0, 0, tiled=True)  75.3 us
    all_to_all x1, blocking collectives, per_device(): lax.all_to_all(send.reshape(experts, 2 * capacity, width), 'expert', 0, 0...  69.4 us
    all_to_all x1, starting transfers between devices, per_device(): partials = lax.all_to_all(partial, 'dp', 0, 0, tiled=True)  37.1 us
    all_to_all x1, waiting for transfers between devices, per_device(): lax.all_to_all(back.reshape(experts, padded, width), 'expert', 0, 0, tile...  29.1 us
    pallas_call x1, Pallas kernels, per_device(): call(functools.partial(expert_kernel, experts, capacity), 'expert', (shap...  14 us
    pallas_call x1, Pallas kernels, per_device(): call(functools.partial(gram_kernel, replicas), 'gram', shape((replicas, r...  8.49 us
    all_to_all x1, starting transfers between devices, per_device(): arrived = lax.all_to_all(blocks, 'dp', 0, 0, tiled=True)  7.75 us
    unnamed x24, local copies, waits for them, and re-layouts  6.2 us
  transfers between devices with their start and end apart: 3, of which 3 were waited for; matrix products, arithmetic and copies ran while one was open for 0% of the time, Pallas kernels for 5%

profile of v1, /device:TPU:2, one launch (start us, length us, event | category | flops | bytes accessed | tf_op | source)
XLA Modules:
  0.0 268.6 jit_solution(7385373522767408236)
XLA Ops:
  0.6 1.0 copy-done.3
  1.7 1.0 copy-done.4
  2.7 0.7 copy-done.8
  3.4 0.7 copy-done.10
  4.1 1.0 dispatch.1
  5.1 69.4 %all_to_all.20 = bf16[16,40,2048]{2,1,0:T(8,128)(2,1)} all-to-all(bf16[16,40,2048]{2,1,0:T(8,128)(2,1)S(1)} %bitcast.13), channel_id=1, replica_groups=mesh['dp'=16,'expert'=16] {'expert'}, dimensions={0} | all-to-all | bytes 5242880 | tf_op jit(solution)/shard_map/all_to_all | solution.py:297
  74.5 14.0 %expert.1 = (bf16[16,1536,128]{2,1,0:T(8,128)(2,1)}, bf16[320,512]{1,0:T(8,128)(2,1)}, bf16[320,512]{1,0:T(8,128)(2,1)}, f32[320,128]{1,0:T(8,128)}) custom-call(bf16[640,2048]{1,0:T(8,128)(2,1)} %bitcast.24, bf16[2048,512]{1,0:T(8,128)(2,1)} %bitcast.14, bf16[2048,512]{1,0:T(8,128)(2,1)} %bitcast.16, bf16[512,2048]{1,0:T(8,128)(2,1)} %bitcast.25), custom_call_target="tpu_custom_call" | custom-call | tf_op jit(solution)/shard_map/expert/pallas_call | solution.py:300
  88.5 0.0 copy-start.7
  88.6 7.8 %all-to-all-start.1 = ((bf16[16,1536,128]{2,1,0:T(8,128)(2,1)}), bf16[16,1536,128]{2,1,0:T(8,128)(2,1)}, u32[]{:S(2)}, u32[]{:S(2)}) async-start(bf16[16,1536,128]{2,1,0:T(8,128)(2,1)} %get-tuple-element.14), calls=%async_computation.1 | async-start | bytes 12582912 | tf_op jit(solution)/shard_map/all_to_all | solution.py:312
  96.3 0.0 copy-start.1
  96.4 1.6 copy-done.1
  97.9 3.0 %return_rows.1 = bf16[384,2048]{1,0:T(8,128)(2,1)S(1)} custom-call(bf16[320,512]{1,0:T(8,128)(2,1)S(1)} %copy-done.5, bf16[320,512]{1,0:T(8,128)(2,1)S(1)} %copy-done.6, f32[320,128]{1,0:T(8,128)S(1)} %copy-done.7, bf16[2048,512]{1,0:T(8,128)(2,1)S(1)} %bitcast.15, bf16[2048,512]{1,0:T(8,128)(2,1)S(1)} %bitcast.17), custom_call_target="tpu_custom_call" | custom-call | tf_op jit(solution)/shard_map/return_rows/pallas_call | solution.py:313
  101.0 0.0 copy-start.2
  101.0 1.2 copy-done.2
  102.2 75.3 %all-to-all-done.1.arrived_ref = bf16[16,1536,128]{2,1,0:T(8,128)(2,1)} async-done(((bf16[16,1536,128]{2,1,0:T(8,128)(2,1)}), bf16[16,1536,128]{2,1,0:T(8,128)(2,1)}, u32[]{:S(2)}, u32[]{:S(2)}) %all-to-all-start.1) | async-done | bytes 6291488 | tf_op jit(solution)/shard_map/all_to_all | solution.py:312
  177.5 3.9 %all-to-all-start.3 = ((bf16[16,24,2048]{2,1,0:T(8,128)(2,1)}), bf16[16,24,2048]{2,1,0:T(8,128)(2,1)S(1)}, u32[]{:S(2)}, u32[]{:S(2)}) async-start(bf16[16,24,2048]{2,1,0:T(8,128)(2,1)} %bitcast.19), calls=%async_computation.3 | async-start | bytes 3145728 | tf_op jit(solution)/shard_map/all_to_all | solution.py:317
  181.4 0.0 copy-start.9
  181.4 0.0 copy-start.11
  181.4 8.5 %gram.1 = f32[16,16,128]{2,1,0:T(8,128)} custom-call(bf16[16,1536,128]{2,1,0:T(8,128)(2,1)} %all-to-all-done.1.arrived_ref), custom_call_target="tpu_custom_call" | custom-call | tf_op jit(solution)/shard_map/gram/pallas_call | solution.py:326
  189.9 29.1 %all-to-all-done.3 = bf16[16,24,2048]{2,1,0:T(8,128)(2,1)S(1)} async-done(((bf16[16,24,2048]{2,1,0:T(8,128)(2,1)}), bf16[16,24,2048]{2,1,0:T(8,128)(2,1)S(1)}, u32[]{:S(2)}, u32[]{:S(2)}) %all-to-all-start.3) | async-done | bytes 1572896 | tf_op jit(solution)/shard_map/all_to_all | solution.py:317
  219.1 37.1 %all-to-all-start.2 = ((f32[16,16,128]{2,1,0:T(8,128)}), f32[16,16,128]{2,1,0:T(8,128)S(1)}, u32[]{:S(2)}, u32[]{:S(2)}) async-start(f32[16,16,128]{2,1,0:T(8,128)} %gram.1), calls=%async_computation.2 | async-start | bytes 262144 | tf_op jit(solution)/shard_map/all_to_all | solution.py:330
  256.2 1.5 gather_back.1
  257.6 5.3 %all-to-all-done.2.partial_ref = f32[16,16,128]{2,1,0:T(8,128)S(1)} async-done(((f32[16,16,128]{2,1,0:T(8,128)}), f32[16,16,128]{2,1,0:T(8,128)S(1)}, u32[]{:S(2)}, u32[]{:S(2)}) %all-to-all-start.2) | async-done | bytes 131104 | tf_op jit(solution)/shard_map/all_to_all | solution.py:330
  263.0 5.7 %combine.1 = (f32[128,512]{1,0:T(8,128)}, f32[128,512]{1,0:T(8,128)}, f32[512,128]{1,0:T(8,128)}) custom-call(f32[16,16,128]{2,1,0:T(8,128)S(1)} %all-to-all-done.2.partial_ref, bf16[16,1536,128]{2,1,0:T(8,128)(2,1)} %all-to-all-done.1.arrived_ref), custom_call_target="tpu_custom_call" | custom-call | tf_op jit(solution)/shard_map/combine/pallas_call | solution.py:331
  (13 shorter events, 0.0 us)
Async XLA Ops:
  0.6 1.0 copy-start.3
  1.7 1.0 copy-start.4
  2.7 0.7 copy-start.8
  3.4 0.7 copy-start.10
  88.5 7.8 %copy-start = (bf16[1,2048,512]{2,1,0:T(8,128)(2,1)S(1)}, bf16[1,2048,512]{2,1,0:T(8,128)(2,1)}, u32[]{:S(2)}) copy-start(bf16[1,2048,512]{2,1,0:T(8,128)(2,1)} %param.11) | copy-start | bytes 6291460
  88.5 7.8 %copy-start.5 = (bf16[320,512]{1,0:T(8,128)(2,1)S(1)}, bf16[320,512]{1,0:T(8,128)(2,1)}, u32[]{:S(2)}) copy-start(bf16[320,512]{1,0:T(8,128)(2,1)} %get-tuple-element.18.gate_grad_ref) | copy-start | bytes 983044
  88.5 7.8 %copy-start.6 = (bf16[320,512]{1,0:T(8,128)(2,1)S(1)}, bf16[320,512]{1,0:T(8,128)(2,1)}, u32[]{:S(2)}) copy-start(bf16[320,512]{1,0:T(8,128)(2,1)} %get-tuple-element.19.up_grad_ref) | copy-start | bytes 983044
  88.5 7.8 %copy-start.7 = (f32[320,128]{1,0:T(8,128)S(1)}, f32[320,128]{1,0:T(8,128)}, u32[]{:S(2)}) copy-start(f32[320,128]{1,0:T(8,128)} %get-tuple-element.20.router_ref) | copy-start | bytes 491524
  88.6 89.0 %all-to-all-start.1 = ((bf16[16,1536,128]{2,1,0:T(8,128)(2,1)}), bf16[16,1536,128]{2,1,0:T(8,128)(2,1)}, u32[]{:S(2)}, u32[]{:S(2)}) async-start(bf16[16,1536,128]{2,1,0:T(8,128)(2,1)} %get-tuple-element.14), calls=%async_computation.1 | async-start | bytes 12582912 | tf_op jit(solution)/shard_map/all_to_all | solution.py:312
  96.3 1.6 copy-start.1
  101.0 1.2 copy-start.2
  177.5 41.5 %all-to-all-start.3 = ((bf16[16,24,2048]{2,1,0:T(8,128)(2,1)}), bf16[16,24,2048]{2,1,0:T(8,128)(2,1)S(1)}, u32[]{:S(2)}, u32[]{:S(2)}) async-start(bf16[16,24,2048]{2,1,0:T(8,128)(2,1)} %bitcast.19), calls=%async_computation.3 | async-start | bytes 3145728 | tf_op jit(solution)/shard_map/all_to_all | solution.py:317
  181.4 74.8 %copy-start.9 = (s32[128,2]{0,1:T(2,128)S(1)}, s32[128,2]{0,1:T(2,128)}, u32[]{:S(2)}) copy-start(s32[128,2]{0,1:T(2,128)} %param.8) | copy-start | bytes 3076
  181.4 74.7 %copy-start.11 = (bf16[128,2]{0,1:T(2,128)(2,1)S(1)}, bf16[128,2]{0,1:T(2,128)(2,1)}, u32[]{:S(2)}) copy-start(bf16[128,2]{0,1:T(2,128)(2,1)} %param.9) | copy-start | bytes 1540
  219.1 43.9 %all-to-all-start.2 = ((f32[16,16,128]{2,1,0:T(8,128)}), f32[16,16,128]{2,1,0:T(8,128)S(1)}, u32[]{:S(2)}, u32[]{:S(2)}) async-start(f32[16,16,128]{2,1,0:T(8,128)} %gram.1), calls=%async_computation.2 | async-start | bytes 262144 | tf_op jit(solution)/shard_map/all_to_all | solution.py:330

commit v2 on v1

v2 whole, which is shorter than its diff:
```python
import functools

import jax
import jax.numpy as jnp
from jax import lax
from jax.experimental import pallas as pl
from jax.experimental.pallas import tpu as pltpu
from jax.sharding import PartitionSpec as P

epsilon = 1e-06
VMEM = pl.BlockSpec(memory_space=pltpu.VMEM)
F32 = jnp.float32
BF16 = jnp.bfloat16


def params(mib):
    return pltpu.CompilerParams(vmem_limit_bytes=mib << 20)


def iota(shape, dim):
    return lax.broadcasted_iota(jnp.int32, shape, dim)


def quotient(value, divisor, limit):
    factor = -(-(1 << 20) // divisor)
    assert all((v * factor) >> 20 == v // divisor for v in range(limit))
    return (value * factor) >> 20


def flag(condition):
    return jnp.where(condition, 1.0, 0.0)


def matmul(a, b, a_dim=1, b_dim=0, precision=None):
    return lax.dot_general(
        a, b, (((a_dim,), (b_dim,)), ((), ())), precision=precision, preferred_element_type=F32
    )


def occupants(first_choice, second_choice, expert_of, slot_of, tokens):
    first = flag(first_choice == expert_of)
    second = flag(second_choice == expert_of)
    named = first + second
    shape = (tokens, tokens)
    earlier = flag(iota(shape, 0) < iota(shape, 1)).astype(BF16)
    count = matmul(named.astype(BF16), earlier)
    taken = named * flag(count == slot_of.astype(F32))
    return taken, first, second


def dispatch_kernel(
    capacity, routing_ref, probs_ref, tokens_ref, cot_ref, out_ref, both_ref, token_sem, cot_sem
):
    tokens, width = tokens_ref.shape
    token_copy = pltpu.make_async_copy(tokens_ref, both_ref.at[0:tokens, :], token_sem)
    cot_copy = pltpu.make_async_copy(cot_ref, both_ref.at[tokens : 2 * tokens, :], cot_sem)
    token_copy.start()
    cot_copy.start()
    rows = out_ref.shape[0]
    row = iota((rows, tokens), 0)
    expert_of = quotient(row, 2 * capacity, rows)
    place = row - expert_of * (2 * capacity)
    is_cot = flag(place >= capacity)
    slot_of = jnp.where(place >= capacity, place - capacity, place)
    routing = routing_ref[...]
    taken, first, second = occupants(routing[0:1, :], routing[1:2, :], expert_of, slot_of, tokens)
    probs = probs_ref[...].astype(F32)
    weight = first * probs[0:1, :] + second * probs[1:2, :]
    pick = jnp.concatenate(
        [(taken * (1.0 - is_cot)).astype(BF16), (taken * is_cot * weight).astype(BF16)], axis=1
    )
    token_copy.wait()
    cot_copy.wait()
    step = 512
    for at in range(0, width, step):
        out_ref[:, at : at + step] = matmul(pick, both_ref[:, at : at + step]).astype(BF16)
    out_ref[:, width:] = (taken * (1.0 - is_cot + is_cot * first)).astype(BF16)


def expert_kernel(
    blocks, capacity, mixed_ref, gate_ref, up_ref, down_ref,
    blocks_ref, back_ref, routed_ref, scaled_ref, rows_grad_ref, out_ref, made_ref, out_sem, made_sem,
):
    slots, width = routed_ref.shape
    hidden_width = gate_ref.shape[1]
    rows = mixed_ref.shape[0]
    step = 512
    for e in range(blocks):
        into = slice(e * capacity, (e + 1) * capacity)
        routed_ref[into, :] = mixed_ref[2 * e * capacity : (2 * e + 1) * capacity, 0:width]
        scaled_ref[into, :] = mixed_ref[(2 * e + 1) * capacity : (2 * e + 2) * capacity, 0:width]
    routed = routed_ref[...]
    scaled = scaled_ref[...]
    gate_pre = matmul(routed, gate_ref[...])
    up_pre = matmul(routed, up_ref[...])
    hidden_grad = matmul(scaled, down_ref[...], 1, 1)
    sigmoid = 1.0 / (1.0 + jnp.exp(-gate_pre))
    activated = gate_pre * sigmoid
    hidden = (activated * up_pre).astype(BF16)
    up_grad = (hidden_grad * activated).astype(BF16)
    gate_grad = (hidden_grad * up_pre * sigmoid * (1.0 + gate_pre * (1.0 - sigmoid))).astype(BF16)
    dots = jnp.sum(hidden.astype(F32) * hidden_grad, axis=1, keepdims=True)
    for at in range(0, width, step):
        rows_grad_ref[:, at : at + step] = (
            matmul(gate_grad, gate_ref[at : at + step, :], 1, 1)
            + matmul(up_grad, up_ref[at : at + step, :], 1, 1)
        ).astype(BF16)
    part = mixed_ref[:, width:]
    tokens = part.shape[1]
    slot = iota((slots, rows), 0)
    source = slot + quotient(slot, capacity, slots) * capacity
    column = iota((slots, rows), 1)
    taken = matmul(flag(column == source).astype(BF16), part)
    first = matmul(flag(column == source + capacity).astype(BF16), part)
    second = taken - first
    block_of = quotient(iota((slots, tokens), 0), capacity, slots)
    dot_rows = []
    for which in (first, second):
        value = which * dots
        high = value.astype(BF16).astype(F32)
        dot_rows.append((high, value - high))
    window = 32
    slots_out = out_ref.shape[0]
    copies = []
    for e in range(blocks):
        start = (capacity * e) // 16 * 16
        mine = flag(block_of[start : start + window, :] == e)
        place = (taken[start : start + window, :] * mine).T.astype(BF16)
        turn = e % slots_out
        if e >= slots_out:
            copies[e - slots_out].wait()
        for at in range(0, width, step):
            out_ref[turn, 0:tokens, at : at + step] = matmul(
                place, rows_grad_ref[start : start + window, at : at + step]
            ).astype(BF16)
        extra = [
            jnp.sum(dot_rows[which][part][start : start + window, :] * mine, axis=0, keepdims=True)
            for part in (0, 1)
            for which in (0, 1)
        ]
        extra = jnp.concatenate(extra + [jnp.zeros((4, tokens), F32)], axis=0)
        extra = jnp.concatenate([extra, jnp.zeros((8, width - tokens), F32)], axis=1)
        out_ref[turn, tokens : tokens + 8, :] = extra.astype(BF16)
        copy = pltpu.make_async_copy(out_ref.at[turn], back_ref.at[e], out_sem.at[turn])
        copy.start()
        copies.append(copy)
    shard = blocks_ref.shape[2]
    scaling = 1.0 / slots
    step = 4 * shard
    made = []
    for m, (left, right_ref) in enumerate(
        ((gate_grad, routed_ref), (up_grad, routed_ref), (hidden, scaled_ref))
    ):
        left_t = left.T
        for at in range(0, width, step):
            grads = (matmul(left_t, right_ref[:, at : at + step]) * scaling).astype(BF16)
            for j in range(step // shard):
                made_ref[at // shard + j, m * hidden_width : (m + 1) * hidden_width, :] = grads[
                    :, j * shard : (j + 1) * shard
                ]
            piece = (
                slice(at // shard, (at + step) // shard),
                slice(m * hidden_width, (m + 1) * hidden_width),
            )
            copy = pltpu.make_async_copy(
                made_ref.at[piece], blocks_ref.at[piece], made_sem.at[len(made)]
            )
            copy.start()
            made.append(copy)
    for copy in copies[-slots_out:] + made:
        copy.wait()


def gram_kernel(replicas, arrived_ref, out_ref):
    kinds = 3
    hidden_width = arrived_ref.shape[1] // kinds
    lanes = arrived_ref.shape[2]
    group = 16
    rows = replicas * group
    square = (rows, rows)
    same = flag((iota(square, 0) & (group - 1)) == (iota(square, 1) & (group - 1)))
    member = flag((iota((rows, lanes), 0) >> 4) == iota((rows, lanes), 1))
    fold = flag((iota((replicas, rows), 1) >> 4) == iota((replicas, rows), 0))
    result = jnp.zeros((replicas, lanes), F32)
    for m in range(kinds):
        pieces = [
            arrived_ref[:, at : at + group, :].reshape(rows, lanes)
            for at in range(m * hidden_width, (m + 1) * hidden_width, group)
        ]
        pieces = jnp.concatenate(pieces, axis=1)
        total = matmul(pieces, pieces, 1, 1)
        folded = matmul(total * same, member, precision=lax.Precision.HIGHEST)
        gram = matmul(fold, folded, precision=lax.Precision.HIGHEST)
        result = result + (pltpu.roll(gram, m * replicas, 1) if m else gram)
    for j in range(out_ref.shape[0]):
        out_ref[j] = result


def combine_kernel(
    replicas, partial_ref, arrived_hbm, back_hbm, probs_ref, gate_ref, up_ref, down_ref, grad_hbm, router_ref,
    arrived_ref, back_ref, arrived_sem, back_sem, grad_sem,
):
    tokens = grad_hbm.shape[0]
    third = arrived_hbm.shape[1] // 3
    loads = []
    for m in range(3):
        piece = (slice(None), slice(m * third, (m + 1) * third))
        loads.append(pltpu.make_async_copy(arrived_hbm.at[piece], arrived_ref.at[piece], arrived_sem.at[m]))
        loads[m].start()
    back_copy = pltpu.make_async_copy(back_hbm, back_ref, back_sem)
    back_copy.start()
    kinds = 3
    lanes = partial_ref.shape[2]
    hidden_width = arrived_ref.shape[1] // kinds
    summed = partial_ref[0]
    for j in range(1, partial_ref.shape[0]):
        summed = summed + partial_ref[j]
    row = iota((replicas, lanes), 0)
    lane = iota((replicas, lanes), 1)
    diagonal = flag(row == lane)
    inside = flag(lane < replicas)
    for m in range(kinds):
        gram = (pltpu.roll(summed, lanes - m * replicas, 1) if m else summed) * inside
        weights = diagonal
        half = replicas // 2
        while half >= 1:
            across = pltpu.roll(gram, lanes - half, 1)
            below = pltpu.roll(gram, replicas - half, 0)
            corner = pltpu.roll(across, replicas - half, 0)
            coefs = []
            for axis in (0, 1):
                former_sq = jnp.sum(gram * diagonal, axis=axis, keepdims=True)
                latter_sq = jnp.sum(corner * diagonal, axis=axis, keepdims=True)
                inner_sum = jnp.sum(across * diagonal, axis=axis, keepdims=True)
                former_sq = jnp.maximum(former_sq, 0.0)
                latter_sq = jnp.maximum(latter_sq, 0.0)
                coefs.append(
                    (
                        1.0 - inner_sum / (2.0 * (former_sq + epsilon)),
                        1.0 - inner_sum / (2.0 * (latter_sq + epsilon)),
                    )
                )
            (former_row, latter_row), (former_col, latter_col) = coefs
            live = flag(row < half) * flag(lane < half)
            gram = live * (
                former_col * (gram * former_row + across * latter_row)
                + latter_col * (below * former_row + corner * latter_row)
            )
            weights = flag(row < half) * (
                former_col * weights + latter_col * pltpu.roll(weights, replicas - half, 0)
            )
            half //= 2
        scalars = [
            jnp.sum(weights * flag(lane == d), axis=(0, 1), keepdims=True) for d in range(replicas)
        ]
        if m == 0:
            back_copy.wait()
            grad_copy = pltpu.make_async_copy(back_ref.at[0:tokens, :], grad_hbm, grad_sem)
            grad_copy.start()
        loads[m].wait()
        step = 128
        for at in range(0, hidden_width, step):
            start = m * hidden_width + at
            total = scalars[0] * arrived_ref[0, start : start + step, :].astype(F32)
            for d in range(1, replicas):
                total = total + scalars[d] * arrived_ref[d, start : start + step, :].astype(F32)
            if m == 2:
                down_ref[at : at + step, :] = total
            else:
                (gate_ref, up_ref)[m][:, at : at + step] = total.T
    dots = back_ref[tokens : tokens + 8, 0:tokens].astype(F32)
    router_ref[...] = ((dots[0:2, :] + dots[2:4, :]) / probs_ref[...].astype(F32)).astype(BF16)
    grad_copy.wait()


def call(kernel, name, out_shapes, mib, scratch=(), specs=None, out_specs=None):
    more = {}
    if specs is not None:
        more["in_specs"] = specs
    if out_specs is not None:
        more["out_specs"] = out_specs
    return pl.pallas_call(
        kernel,
        name=name,
        out_shape=out_shapes,
        scratch_shapes=scratch,
        compiler_params=params(mib),
        **more,
    )


def per_device(tokens, routing, probs, cotangent, w_gate, w_up, w_down):
    experts = lax.axis_size("expert")
    replicas = lax.axis_size("dp")
    rows_here, top_count = routing.shape
    width = tokens.shape[1]
    hidden_width = w_gate.shape[2]
    capacity = 5 * rows_here * top_count // (4 * experts)
    slots = experts * capacity
    shard = width // replicas
    shape = jax.ShapeDtypeStruct
    routing_rows = routing.T
    prob_rows = probs.T
    gate, up, down = w_gate[0], w_up[0], w_down[0]
    pinned = functools.partial(pltpu.with_memory_space_constraint, memory_space=pltpu.HBM)
    in_hbm = pl.BlockSpec(memory_space=pltpu.HBM)
    dma = pltpu.SemaphoreType.DMA

    send = call(
        functools.partial(dispatch_kernel, capacity),
        "dispatch", shape((2 * slots, width + rows_here), BF16), 16,
        (pltpu.VMEM((2 * rows_here, width), BF16), dma, dma),
        specs=[VMEM, VMEM, in_hbm, in_hbm],
    )(routing_rows, prob_rows, pinned(tokens), pinned(cotangent))
    mixed = lax.all_to_all(
        send.reshape(experts, 2 * capacity, width + rows_here), "expert", 0, 0, tiled=True
    ).reshape(2 * slots, width + rows_here)
    blocks, back = call(
        functools.partial(expert_kernel, experts, capacity),
        "expert",
        (
            pltpu.HBM((replicas, 3 * hidden_width, shard), BF16),
            pltpu.HBM((experts, rows_here + 8, width), BF16),
        ),
        36,
        (
            pltpu.VMEM((slots, width), BF16),
            pltpu.VMEM((slots, width), BF16),
            pltpu.VMEM((slots, width), BF16),
            pltpu.VMEM((4, rows_here + 8, width), BF16),
            pltpu.VMEM((replicas, 3 * hidden_width, shard), BF16),
            dma((4,)),
            dma((3 * width // 512,)),
        ),
        specs=[VMEM] * 4,
        out_specs=(in_hbm, in_hbm),
    )(mixed, gate, up, down)
    back = lax.psum_scatter(
        back.reshape(experts * (rows_here + 8), width), "expert", scatter_dimension=0, tiled=True
    )
    arrived = lax.all_to_all(blocks, "dp", 0, 0, tiled=True)
    partial = call(
        functools.partial(gram_kernel, replicas),
        "gram", shape((replicas, replicas, 128), F32), 20,
    )(arrived)
    partials = lax.all_to_all(partial, "dp", 0, 0, tiled=True)
    grad_gate, grad_up, grad_down, input_grad, router_grad = call(
        functools.partial(combine_kernel, replicas),
        "combine",
        (
            shape((shard, hidden_width), F32),
            shape((shard, hidden_width), F32),
            shape((hidden_width, shard), F32),
            pltpu.HBM((rows_here, width), BF16),
            shape((top_count, rows_here), BF16),
        ),
        16,
        (
            pltpu.VMEM((replicas, 3 * hidden_width, shard), BF16),
            pltpu.VMEM((rows_here + 8, width), BF16),
            dma((3,)),
            dma,
            dma,
        ),
        specs=[VMEM, in_hbm, in_hbm, VMEM],
        out_specs=(VMEM, VMEM, VMEM, in_hbm, VMEM),
    )(partials, pinned(arrived), pinned(back), prob_rows)
    return (grad_gate[None], grad_up[None], grad_down[None], input_grad, router_grad.T)


def solution(mesh):
    placed = (
        P(("dp", "expert"), None),
        P(("dp", "expert"), None),
        P(("dp", "expert"), None),
        P(("dp", "expert"), None),
        P("expert", None, None),
        P("expert", None, None),
        P("expert", None, None),
    )
    return jax.shard_map(
        per_device,
        mesh=mesh,
        in_specs=placed,
        out_specs=(
            P("expert", "dp", None),
            P("expert", "dp", None),
            P("expert", None, "dp"),
            P(("dp", "expert"), None),
            P(("dp", "expert"), None),
        ),
        check_vma=False,
    )
```

time: 271 us -> 208 us (0.77)
  waiting for transfers between devices: 110 us -> 0.02 us
  blocking collectives: 69.4 us -> 166 us
  starting transfers between devices: 48.8 us -> 0.04 us
  between operations: 0.76 us -> 14.1 us
  Pallas kernels: 33.7 us -> 26.5 us
  local copies, waits for them, and re-layouts: 6.2 us -> 1.35 us
    all_to_all x3 -> x0, waiting for transfers between devices: 110 us -> none  [the longest x1 75.3 us: per_device(): arrived = lax.all_to_all(blocks, 'dp', 0, 0, tiled=True)]
    all_to_all x1 -> x3, blocking collectives: 69.4 us -> 166 us  [the longest x1 79.5 us: per_device(): arrived = lax.all_to_all(blocks, 'dp', 0, 0, tiled=True)]
    all_to_all x3 -> x0, starting transfers between devices: 48.8 us -> none  [the longest x1 37.1 us: per_device(): partials = lax.all_to_all(partial, 'dp', 0, 0, tiled=True)]
    unnamed x24 -> x14, local copies, waits for them, and re-layouts: 6.2 us -> 1.35 us
    pallas_call x4 -> x2, Pallas kernels: 19.5 us -> 15 us  [the longest x1 12.7 us: per_device(): call(functools.partial(expert_kernel, experts, capacity), 'expert', (pltp...]
    pallas_call x1, Pallas kernels: 8.49 us -> 5.03 us  [per_device(): call(functools.partial(gram_kernel, replicas), 'gram', shape((replicas, r...]
  transfers between devices with their start and end apart: 3 -> 1, of which waited for: 3 -> 0; matrix products, arithmetic and copies ran while one was open for 0% -> 0% of each run, Pallas kernels for 5% -> 2%
where the time goes in v2:
time: 208 us
  blocking collectives  166 us (80%)
  Pallas kernels  26.5 us (13%)
  between operations  14.1 us (7%)
    all_to_all x1, blocking collectives, per_device(): arrived = lax.all_to_all(blocks, 'dp', 0, 0, tiled=True)  79.5 us
    all_to_all x1, blocking collectives, per_device(): lax.all_to_all(send.reshape(experts, 2 * capacity, width + rows_here), 'e...  74 us
    pallas_call x1, Pallas kernels, per_device(): call(functools.partial(expert_kernel, experts, capacity), 'expert', (pltp...  12.7 us
    all_to_all x1, blocking collectives, per_device(): partials = lax.all_to_all(partial, 'dp', 0, 0, tiled=True)  12 us
    pallas_call x1, Pallas kernels, per_device(): call(functools.partial(combine_kernel, replicas), 'combine', (shape((shar...  6.4 us
    pallas_call x1, Pallas kernels, per_device(): call(functools.partial(gram_kernel, replicas), 'gram', shape((replicas, r...  5.03 us
  transfers between devices with their start and end apart: 1, of which 0 were waited for; matrix products, arithmetic and copies ran while one was open for 0% of the time, Pallas kernels for 2%

profile of v2, /device:TPU:2, one launch (start us, length us, event | category | flops | bytes accessed | tf_op | source)
XLA Modules:
  0.0 207.5 jit_solution(6097346270504309950)
XLA Ops:
  7.2 0.0 reduce-scatter.2.cloned.1.call-start
  7.2 0.0 copy-start.4
  7.2 0.6 copy-done.4
  7.9 0.0 copy-start.6
  7.9 0.7 copy-done.6
  8.6 0.0 copy-start.3
  8.6 2.4 %dispatch.1 = bf16[640,2176]{1,0:T(8,128)(2,1)S(1)} custom-call(s32[2,128]{1,0:T(2,128)S(1)} %bitcast.19, bf16[2,128]{1,0:T(2,128)(2,1)S(1)} %bitcast.17, bf16[128,2048]{1,0:T(8,128)(2,1)} %tokens_ref.1, bf16[128,2048]{1,0:T(8,128)(2,1)} %cot_ref.1), custom_call_target="tpu_custom_call" | custom-call | tf_op jit(solution)/shard_map/dispatch/pallas_call | solution.py:309
  10.9 0.0 copy-start.1
  10.9 0.0 copy-start.2
  10.9 74.0 %all_to_all.15 = bf16[16,40,2176]{2,1,0:T(8,128)(2,1)S(1)} all-to-all(bf16[16,40,2176]{2,1,0:T(8,128)(2,1)S(1)} %bitcast.13), channel_id=1, replica_groups=mesh['dp'=16,'expert'=16] {'expert'}, dimensions={0} | all-to-all | bytes 5570560 | tf_op jit(solution)/shard_map/all_to_all | solution.py:315
  85.0 0.0 copy-done.3
  85.0 0.0 copy-done.1
  85.0 0.0 copy-done.2
  85.0 12.7 %expert.1 = (bf16[16,1536,128]{2,1,0:T(8,128)(2,1)}, bf16[16,136,2048]{2,1,0:T(8,128)(2,1)}) custom-call(bf16[640,2176]{1,0:T(8,128)(2,1)S(1)} %bitcast.12, bf16[2048,512]{1,0:T(8,128)(2,1)S(1)} %bitcast.14, bf16[2048,512]{1,0:T(8,128)(2,1)S(1)} %bitcast.15, bf16[512,2048]{1,0:T(8,128)(2,1)S(1)} %bitcast.16), custom_call_target="tpu_custom_call" | custom-call | tf_op jit(solution)/shard_map/expert/pallas_call | solution.py:318
  97.6 0.0 reduce-scatter.2.cloned.1.call-update
  97.7 79.5 %all_to_all.16.arrived_ref.arrived_hbm = bf16[16,1536,128]{2,1,0:T(8,128)(2,1)S(1)} all-to-all(bf16[16,1536,128]{2,1,0:T(8,128)(2,1)} %get-tuple-element.12), channel_id=1, replica_groups=mesh['dp'=16,'expert'=16] {'dp'}, dimensions={0} | all-to-all | bytes 12582912 | tf_op jit(solution)/shard_map/all_to_all | solution.py:341
  177.1 0.0 copy-start
  177.1 0.0 copy-start.5
  177.1 5.0 %gram.1 = f32[16,16,128]{2,1,0:T(8,128)S(1)} custom-call(bf16[16,1536,128]{2,1,0:T(8,128)(2,1)S(1)} %all_to_all.16.arrived_ref.arrived_hbm), custom_call_target="tpu_custom_call" | custom-call | tf_op jit(solution)/shard_map/gram/pallas_call | solution.py:342
  182.2 0.0 copy-done
  182.2 12.0 %all_to_all.17.partial_ref = f32[16,16,128]{2,1,0:T(8,128)S(1)} all-to-all(f32[16,16,128]{2,1,0:T(8,128)S(1)} %gram.1), channel_id=1, replica_groups=mesh['dp'=16,'expert'=16] {'dp'}, dimensions={0} | all-to-all | bytes 262144 | tf_op jit(solution)/shard_map/all_to_all | solution.py:346
  194.2 0.0 reduce-scatter.2.cloned.1.call-done.back_hbm
  194.2 0.0 copy-done.5
  194.2 6.4 %combine.1 = (f32[128,512]{1,0:T(8,128)}, f32[128,512]{1,0:T(8,128)}, f32[512,128]{1,0:T(8,128)}, bf16[128,2048]{1,0:T(8,128)(2,1)}, bf16[2,128]{1,0:T(2,128)(2,1)}) custom-call(f32[16,16,128]{2,1,0:T(8,128)S(1)} %all_to_all.17.partial_ref, bf16[16,1536,128]{2,1,0:T(8,128)(2,1)} %copy-done, bf16[136,2048]{1,0:T(8,128)(2,1)} %reduce-scatter.2.cloned.1.call-done.back_hbm, ...), custom_call_target="tpu_custom_call" | custom-call | tf_op jit(solution)/shard_map/combine/pallas_call | solution.py:347
Async XLA Ops:
  7.2 187.1 %reduce-scatter.2.cloned.1.call-start = ((), (), s32[]{:S(2)}) async-start(), calls=%async_computation.4 | async-start | bytes 9469952 | tf_op jit(solution)/shard_map/reduce_scatter | solution.py:338
  7.2 0.7 copy-start.4
  7.9 0.7 copy-start.6
  8.6 76.4 %copy-start.3 = (bf16[1,512,2048]{2,1,0:T(8,128)(2,1)S(1)}, bf16[1,512,2048]{2,1,0:T(8,128)(2,1)}, u32[]{:S(2)}) copy-start(bf16[1,512,2048]{2,1,0:T(8,128)(2,1)} %param.13) | copy-start | bytes 6291460
  10.9 74.0 %copy-start.1 = (bf16[1,2048,512]{2,1,0:T(8,128)(2,1)S(1)}, bf16[1,2048,512]{2,1,0:T(8,128)(2,1)}, u32[]{:S(2)}) copy-start(bf16[1,2048,512]{2,1,0:T(8,128)(2,1)} %param.11) | copy-start | bytes 6291460
  10.9 74.0 %copy-start.2 = (bf16[1,2048,512]{2,1,0:T(8,128)(2,1)S(1)}, bf16[1,2048,512]{2,1,0:T(8,128)(2,1)}, u32[]{:S(2)}) copy-start(bf16[1,2048,512]{2,1,0:T(8,128)(2,1)} %param.12) | copy-start | bytes 6291460
  177.1 5.0 %copy-start = (bf16[16,1536,128]{2,1,0:T(8,128)(2,1)}, bf16[16,1536,128]{2,1,0:T(8,128)(2,1)S(1)}, u32[]{:S(2)}) copy-start(bf16[16,1536,128]{2,1,0:T(8,128)(2,1)S(1)} %all_to_all.16.arrived_ref.arrived_hbm) | copy-start | bytes 18874372
  177.1 17.1 %copy-start.5 = (bf16[128,2]{0,1:T(2,128)(2,1)S(1)}, bf16[128,2]{0,1:T(2,128)(2,1)}, u32[]{:S(2)}) copy-start(bf16[128,2]{0,1:T(2,128)(2,1)} %param.9) | copy-start | bytes 1540
Sparse Core Ops, SparseCore 0:
  97.8 70.6 reduce-scatter.1

commit v3 on v2

--- a/solution.py
+++ b/solution.py
@@ -11,6 +11,7 @@
 VMEM = pl.BlockSpec(memory_space=pltpu.VMEM)
 F32 = jnp.float32
 BF16 = jnp.bfloat16
+BACK_STEP = 512
 
 
 def params(mib):
@@ -49,19 +50,38 @@
 
 
 def dispatch_kernel(
-    capacity, routing_ref, probs_ref, tokens_ref, cot_ref, out_ref, both_ref, token_sem, cot_sem
+    capacity, routing_hbm, probs_hbm, tokens_hbm, cot_hbm, out_ref,
+    routing_ref, probs_ref, both_ref, small_sem, wide_sem,
 ):
-    tokens, width = tokens_ref.shape
-    token_copy = pltpu.make_async_copy(tokens_ref, both_ref.at[0:tokens, :], token_sem)
-    cot_copy = pltpu.make_async_copy(cot_ref, both_ref.at[tokens : 2 * tokens, :], cot_sem)
-    token_copy.start()
-    cot_copy.start()
-    rows = out_ref.shape[0]
+    tokens, width = tokens_hbm.shape
+    step = 512
+    routing_copy = pltpu.make_async_copy(routing_hbm, routing_ref, small_sem.at[0])
+    probs_copy = pltpu.make_async_copy(probs_hbm, probs_ref, small_sem.at[1])
+    routing_copy.start()
+    probs_copy.start()
+    copies = []
+    for at in range(0, width, step):
+        pair = []
+        for first_row, source in ((0, tokens_hbm), (tokens, cot_hbm)):
+            pair.append(
+                pltpu.make_async_copy(
+                    source.at[:, at : at + step],
+                    both_ref.at[first_row : first_row + tokens, at : at + step],
+                    wide_sem.at[2 * len(copies) + len(pair)],
+                )
+            )
+            pair[-1].start()
+        copies.append(pair)
+    experts = out_ref.shape[0]
+    pair = 2 * capacity
+    rows = experts * pair
     row = iota((rows, tokens), 0)
-    expert_of = quotient(row, 2 * capacity, rows)
-    place = row - expert_of * (2 * capacity)
+    expert_of = quotient(row, pair, rows)
+    place = row - expert_of * pair
     is_cot = flag(place >= capacity)
     slot_of = jnp.where(place >= capacity, place - capacity, place)
+    routing_copy.wait()
+    probs_copy.wait()
     routing = routing_ref[...]
     taken, first, second = occupants(routing[0:1, :], routing[1:2, :], expert_of, slot_of, tokens)
     probs = probs_ref[...].astype(F32)
@@ -69,26 +89,45 @@
     pick = jnp.concatenate(
         [(taken * (1.0 - is_cot)).astype(BF16), (taken * is_cot * weight).astype(BF16)], axis=1
     )
-    token_copy.wait()
-    cot_copy.wait()
-    step = 512
-    for at in range(0, width, step):
-        out_ref[:, at : at + step] = matmul(pick, both_ref[:, at : at + step]).astype(BF16)
-    out_ref[:, width:] = (taken * (1.0 - is_cot + is_cot * first)).astype(BF16)
+    taken_bf = taken.astype(BF16)
+    counted = (iota((1, tokens), 1) + 1).astype(F32)
+    notes_at = width // tokens * pair
+    out_ref[:, notes_at:, :] = jnp.zeros((experts, 8, tokens), BF16)
+    for k in range(experts):
+        heads = jnp.concatenate(
+            [counted, flag(routing[0:1, :] == k), jnp.zeros((6, tokens), F32)], axis=0
+        ).astype(BF16)
+        notes = matmul(heads, taken_bf[pair * k : pair * (k + 1), :], 1, 1)
+        out_ref[k, notes_at:, 0:pair] = notes.astype(BF16)
+    for at, pair_of_copies in zip(range(0, width, step), copies):
+        for copy in pair_of_copies:
+            copy.wait()
+        sent = matmul(pick, both_ref[:, at : at + step])
+        for c in range(step // tokens):
+            to = (at // tokens + c) * pair
+            for k in range(experts):
+                out_ref[k, to : to + pair, :] = sent[
+                    pair * k : pair * (k + 1), c * tokens : (c + 1) * tokens
+                ].astype(BF16)
 
 
 def expert_kernel(
-    blocks, capacity, mixed_ref, gate_ref, up_ref, down_ref,
+    capacity, mixed_ref, gate_ref, up_ref, down_ref,
     blocks_ref, back_ref, routed_ref, scaled_ref, rows_grad_ref, out_ref, made_ref, out_sem, made_sem,
 ):
     slots, width = routed_ref.shape
     hidden_width = gate_ref.shape[1]
-    rows = mixed_ref.shape[0]
-    step = 512
+    blocks = mixed_ref.shape[0]
+    lanes = mixed_ref.shape[2]
+    tokens = out_ref.shape[1] - 8
+    pair = 2 * capacity
     for e in range(blocks):
         into = slice(e * capacity, (e + 1) * capacity)
-        routed_ref[into, :] = mixed_ref[2 * e * capacity : (2 * e + 1) * capacity, 0:width]
-        scaled_ref[into, :] = mixed_ref[(2 * e + 1) * capacity : (2 * e + 2) * capacity, 0:width]
+        for c in range(width // lanes):
+            columns = slice(c * lanes, (c + 1) * lanes)
+            routed_ref[into, columns] = mixed_ref[e, c * pair : c * pair + capacity, :]
+            scaled_ref[into, columns] = mixed_ref[e, c * pair + capacity : (c + 1) * pair, :]
+    step = 512
     routed = routed_ref[...]
     scaled = scaled_ref[...]
     gate_pre = matmul(routed, gate_ref[...])
@@ -105,69 +144,84 @@
             matmul(gate_grad, gate_ref[at : at + step, :], 1, 1)
             + matmul(up_grad, up_ref[at : at + step, :], 1, 1)
         ).astype(BF16)
-    part = mixed_ref[:, width:]
-    tokens = part.shape[1]
-    slot = iota((slots, rows), 0)
-    source = slot + quotient(slot, capacity, slots) * capacity
-    column = iota((slots, rows), 1)
-    taken = matmul(flag(column == source).astype(BF16), part)
-    first = matmul(flag(column == source + capacity).astype(BF16), part)
+    notes_at = width // lanes * pair
+    notes = mixed_ref[:, notes_at : notes_at + 8, :].astype(F32).reshape(8 * blocks, lanes).astype(BF16)
+    slot = iota((slots, lanes), 0)
+    block_of = quotient(slot, capacity, slots)
+    lane = iota((slots, lanes), 1)
+    own_lane = flag(lane == slot - capacity * block_of)
+    note_col = iota((slots, 8 * blocks), 1)
+    note_block = quotient(iota((slots, 8 * blocks), 0), capacity, slots)
+    named, leading = [
+        jnp.sum(
+            matmul(flag(note_col == 8 * note_block + j).astype(BF16), notes) * own_lane,
+            axis=1, keepdims=True,
+        )
+        for j in (0, 1)
+    ]
+    taken = flag(iota((slots, tokens), 1).astype(F32) + 1.0 == named)
+    first = taken * leading
     second = taken - first
-    block_of = quotient(iota((slots, tokens), 0), capacity, slots)
-    dot_rows = []
-    for which in (first, second):
-        value = which * dots
-        high = value.astype(BF16).astype(F32)
-        dot_rows.append((high, value - high))
-    window = 32
-    slots_out = out_ref.shape[0]
+    high = dots.astype(BF16).astype(F32)
+    low = (dots - high).astype(BF16).astype(F32)
+    extra_row = iota((8 * blocks, slots), 0)
+    extra_same = flag((extra_row >> 3) == quotient(iota((8 * blocks, slots), 1), capacity, slots))
+    extra = jnp.zeros((8 * blocks, tokens), F32)
+    for j, (which, value) in enumerate(((first, high), (second, high), (first, low), (second, low))):
+        extra = extra + matmul(
+            (extra_same * flag((extra_row & 7) == j)).astype(BF16), (which * value).astype(BF16)
+        )
+    out_ref[:, tokens:, :] = jnp.zeros((blocks, 8, width), BF16)
+    for e in range(blocks):
+        out_ref[e, tokens:, 0:tokens] = extra[8 * e : 8 * e + 8, :].astype(BF16)
+    taken_t = taken.T
+    lane_block = quotient(iota((tokens, slots), 1), capacity, slots)
+    split = min(blocks, 256 // capacity)
+    windows = [(0, split, 0, min(slots, 256))]
+    if split < blocks:
+        windows.append((split, blocks, capacity * split // 128 * 128, slots))
+    places = []
+    for low_block, high_block, low_lane, high_lane in windows:
+        lane_part = lane_block[:, low_lane:high_lane]
+        place_part = taken_t[:, low_lane:high_lane]
+        places.append(
+            jnp.concatenate(
+                [(place_part * flag(lane_part == e)).astype(BF16) for e in range(low_block, high_block)],
+                axis=0,
+            )
+        )
     copies = []
-    for e in range(blocks):
-        start = (capacity * e) // 16 * 16
-        mine = flag(block_of[start : start + window, :] == e)
-        place = (taken[start : start + window, :] * mine).T.astype(BF16)
-        turn = e % slots_out
-        if e >= slots_out:
-            copies[e - slots_out].wait()
-        for at in range(0, width, step):
-            out_ref[turn, 0:tokens, at : at + step] = matmul(
-                place, rows_grad_ref[start : start + window, at : at + step]
-            ).astype(BF16)
-        extra = [
-            jnp.sum(dot_rows[which][part][start : start + window, :] * mine, axis=0, keepdims=True)
-            for part in (0, 1)
-            for which in (0, 1)
-        ]
-        extra = jnp.concatenate(extra + [jnp.zeros((4, tokens), F32)], axis=0)
-        extra = jnp.concatenate([extra, jnp.zeros((8, width - tokens), F32)], axis=1)
-        out_ref[turn, tokens : tokens + 8, :] = extra.astype(BF16)
-        copy = pltpu.make_async_copy(out_ref.at[turn], back_ref.at[e], out_sem.at[turn])
+    wide = BACK_STEP
+    for at in range(0, width, wide):
+        columns = slice(at, at + wide)
+        for place, (low_block, high_block, low_lane, high_lane) in zip(places, windows):
+            sent = matmul(place, rows_grad_ref[low_lane:high_lane, columns]).astype(BF16)
+            out_ref[low_block:high_block, 0:tokens, columns] = sent.reshape(
+                high_block - low_block, tokens, wide
+            )
+        copy = pltpu.make_async_copy(
+            out_ref.at[:, :, columns], back_ref.at[:, :, columns], out_sem.at[len(copies)]
+        )
         copy.start()
         copies.append(copy)
     shard = blocks_ref.shape[2]
     scaling = 1.0 / slots
     step = 4 * shard
+    both_t = jnp.concatenate([gate_grad.T, up_grad.T], axis=0)
     made = []
-    for m, (left, right_ref) in enumerate(
-        ((gate_grad, routed_ref), (up_grad, routed_ref), (hidden, scaled_ref))
-    ):
-        left_t = left.T
+    for left, right_ref, row in ((both_t, routed_ref, 0), (hidden.T, scaled_ref, 2 * hidden_width)):
+        tall = left.shape[0]
         for at in range(0, width, step):
-            grads = (matmul(left_t, right_ref[:, at : at + step]) * scaling).astype(BF16)
+            grads = (matmul(left, right_ref[:, at : at + step]) * scaling).astype(BF16)
             for j in range(step // shard):
-                made_ref[at // shard + j, m * hidden_width : (m + 1) * hidden_width, :] = grads[
-                    :, j * shard : (j + 1) * shard
-                ]
-            piece = (
-                slice(at // shard, (at + step) // shard),
-                slice(m * hidden_width, (m + 1) * hidden_width),
-            )
+                made_ref[at // shard + j, row : row + tall, :] = grads[:, j * shard : (j + 1) * shard]
+            piece = (slice(at // shard, (at + step) // shard), slice(row, row + tall))
             copy = pltpu.make_async_copy(
                 made_ref.at[piece], blocks_ref.at[piece], made_sem.at[len(made)]
             )
             copy.start()
             made.append(copy)
-    for copy in copies[-slots_out:] + made:
+    for copy in copies + made:
         copy.wait()
 
 
@@ -206,7 +260,8 @@
     for m in range(3):
         piece = (slice(None), slice(m * third, (m + 1) * third))
         loads.append(pltpu.make_async_copy(arrived_hbm.at[piece], arrived_ref.at[piece], arrived_sem.at[m]))
-        loads[m].start()
+    for load in loads:
+        load.start()
     back_copy = pltpu.make_async_copy(back_hbm, back_ref, back_sem)
     back_copy.start()
     kinds = 3
@@ -253,11 +308,11 @@
         scalars = [
             jnp.sum(weights * flag(lane == d), axis=(0, 1), keepdims=True) for d in range(replicas)
         ]
-        if m == 0:
+        loads[m].wait()
+        if m == 2:
             back_copy.wait()
             grad_copy = pltpu.make_async_copy(back_ref.at[0:tokens, :], grad_hbm, grad_sem)
             grad_copy.start()
-        loads[m].wait()
         step = 128
         for at in range(0, hidden_width, step):
             start = m * hidden_width + at
@@ -298,6 +353,7 @@
     capacity = 5 * rows_here * top_count // (4 * experts)
     slots = experts * capacity
     shard = width // replicas
+    sent_rows = width // rows_here * 2 * capacity + 8
     shape = jax.ShapeDtypeStruct
     routing_rows = routing.T
     prob_rows = probs.T
@@ -308,29 +364,33 @@
 
     send = call(
         functools.partial(dispatch_kernel, capacity),
-        "dispatch", shape((2 * slots, width + rows_here), BF16), 16,
-        (pltpu.VMEM((2 * rows_here, width), BF16), dma, dma),
-        specs=[VMEM, VMEM, in_hbm, in_hbm],
-    )(routing_rows, prob_rows, pinned(tokens), pinned(cotangent))
-    mixed = lax.all_to_all(
-        send.reshape(experts, 2 * capacity, width + rows_here), "expert", 0, 0, tiled=True
-    ).reshape(2 * slots, width + rows_here)
+        "dispatch", shape((experts, sent_rows, rows_here), BF16), 16,
+        (
+            pltpu.VMEM((top_count, rows_here), jnp.int32),
+            pltpu.VMEM((top_count, rows_here), BF16),
+            pltpu.VMEM((2 * rows_here, width), BF16),
+            dma((2,)),
+            dma((width // 256,)),
+        ),
+        specs=[in_hbm] * 4,
+    )(pinned(routing_rows), pinned(prob_rows), pinned(tokens), pinned(cotangent))
+    mixed = lax.all_to_all(send, "expert", 0, 0, tiled=True)
     blocks, back = call(
-        functools.partial(expert_kernel, experts, capacity),
+        functools.partial(expert_kernel, capacity),
         "expert",
         (
             pltpu.HBM((replicas, 3 * hidden_width, shard), BF16),
             pltpu.HBM((experts, rows_here + 8, width), BF16),
         ),
-        36,
+        44,
         (
             pltpu.VMEM((slots, width), BF16),
             pltpu.VMEM((slots, width), BF16),
             pltpu.VMEM((slots, width), BF16),
-            pltpu.VMEM((4, rows_here + 8, width), BF16),
+            pltpu.VMEM((experts, rows_here + 8, width), BF16),
             pltpu.VMEM((replicas, 3 * hidden_width, shard), BF16),
-            dma((4,)),
-            dma((3 * width // 512,)),
+            dma((width // BACK_STEP,)),
+            dma((2 * width // (4 * shard),)),
         ),
         specs=[VMEM] * 4,
         out_specs=(in_hbm, in_hbm),

time: 208 us -> 202 us (0.971)
  blocking collectives: 166 us -> 163 us
where the time goes in v3:
time: 202 us
  blocking collectives  163 us (81%)
  Pallas kernels  24.5 us (12%)
  between operations  14.1 us (7%)
    all_to_all x1, blocking collectives, per_device(): arrived = lax.all_to_all(blocks, 'dp', 0, 0, tiled=True)  78.8 us
    all_to_all x1, blocking collectives, per_device(): mixed = lax.all_to_all(send, 'expert', 0, 0, tiled=True)  72.3 us
    all_to_all x1, blocking collectives, per_device(): partials = lax.all_to_all(partial, 'dp', 0, 0, tiled=True)  11.9 us
    pallas_call x1, Pallas kernels, per_device(): call(functools.partial(expert_kernel, capacity), 'expert', (pltpu.HBM((re...  10.9 us
    pallas_call x1, Pallas kernels, per_device(): call(functools.partial(combine_kernel, replicas), 'combine', (shape((shar...  5.46 us
    pallas_call x1, Pallas kernels, per_device(): call(functools.partial(gram_kernel, replicas), 'gram', shape((replicas, r...  5.03 us
  transfers between devices with their start and end apart: 1, of which 0 were waited for; matrix products, arithmetic and copies ran while one was open for 0% of the time, Pallas kernels for 2%

profile of v3, /device:TPU:2, one launch (start us, length us, event | category | flops | bytes accessed | tf_op | source)
XLA Modules:
  0.0 201.6 jit_solution(17692948660215156818)
XLA Ops:
  7.2 0.0 reduce-scatter.2.cloned.1.call-start
  7.2 0.0 copy-start.3
  7.2 3.0 %dispatch.1 = bf16[16,648,128]{2,1,0:T(8,128)(2,1)S(1)} custom-call(s32[2,128]{1,0:T(2,128)} %bitcast.16, bf16[2,128]{1,0:T(2,128)(2,1)} %bitcast.13, bf16[128,2048]{1,0:T(8,128)(2,1)} %tokens_hbm.1, bf16[128,2048]{1,0:T(8,128)(2,1)} %cot_hbm.1), custom_call_target="tpu_custom_call" | custom-call | tf_op jit(solution)/shard_map/dispatch/pallas_call | solution.py:365
  10.3 0.0 copy-start.1
  10.3 0.0 copy-start.2
  10.3 72.3 %all_to_all.15.mixed_ref = bf16[16,648,128]{2,1,0:T(8,128)(2,1)S(1)} all-to-all(bf16[16,648,128]{2,1,0:T(8,128)(2,1)S(1)} %dispatch.1), channel_id=1, replica_groups=mesh['dp'=16,'expert'=16] {'expert'}, dimensions={0} | all-to-all | bytes 5308416 | tf_op jit(solution)/shard_map/all_to_all | solution.py:377
  82.6 0.0 copy-done.3
  82.6 0.0 copy-done.1
  82.6 0.0 copy-done.2
  82.6 10.9 %expert.1 = (bf16[16,1536,128]{2,1,0:T(8,128)(2,1)}, bf16[16,136,2048]{2,1,0:T(8,128)(2,1)}) custom-call(bf16[16,648,128]{2,1,0:T(8,128)(2,1)S(1)} %all_to_all.15.mixed_ref, bf16[2048,512]{1,0:T(8,128)(2,1)S(1)} %bitcast.10, bf16[2048,512]{1,0:T(8,128)(2,1)S(1)} %bitcast.11, bf16[512,2048]{1,0:T(8,128)(2,1)S(1)} %bitcast.12), custom_call_target="tpu_custom_call" | custom-call | tf_op jit(solution)/shard_map/expert/pallas_call | solution.py:378
  93.5 0.0 reduce-scatter.2.cloned.1.call-update
  93.5 78.8 %all_to_all.16.arrived_ref.arrived_hbm = bf16[16,1536,128]{2,1,0:T(8,128)(2,1)S(1)} all-to-all(bf16[16,1536,128]{2,1,0:T(8,128)(2,1)} %get-tuple-element.12), channel_id=1, replica_groups=mesh['dp'=16,'expert'=16] {'dp'}, dimensions={0} | all-to-all | bytes 12582912 | tf_op jit(solution)/shard_map/all_to_all | solution.py:401
  172.3 0.0 copy-start
  172.3 0.0 copy-start.4
  172.3 5.0 %gram.1 = f32[16,16,128]{2,1,0:T(8,128)S(1)} custom-call(bf16[16,1536,128]{2,1,0:T(8,128)(2,1)S(1)} %all_to_all.16.arrived_ref.arrived_hbm), custom_call_target="tpu_custom_call" | custom-call | tf_op jit(solution)/shard_map/gram/pallas_call | solution.py:402
  177.4 0.0 copy-done
  177.4 11.9 %all_to_all.17.partial_ref = f32[16,16,128]{2,1,0:T(8,128)S(1)} all-to-all(f32[16,16,128]{2,1,0:T(8,128)S(1)} %gram.1), channel_id=1, replica_groups=mesh['dp'=16,'expert'=16] {'dp'}, dimensions={0} | all-to-all | bytes 262144 | tf_op jit(solution)/shard_map/all_to_all | solution.py:406
  189.3 0.0 reduce-scatter.2.cloned.1.call-done.back_hbm
  189.3 0.0 copy-done.4
  189.3 5.5 %combine.1 = (f32[128,512]{1,0:T(8,128)}, f32[128,512]{1,0:T(8,128)}, f32[512,128]{1,0:T(8,128)}, bf16[128,2048]{1,0:T(8,128)(2,1)}, bf16[2,128]{1,0:T(2,128)(2,1)}) custom-call(f32[16,16,128]{2,1,0:T(8,128)S(1)} %all_to_all.17.partial_ref, bf16[16,1536,128]{2,1,0:T(8,128)(2,1)} %copy-done, bf16[136,2048]{1,0:T(8,128)(2,1)} %reduce-scatter.2.cloned.1.call-done.back_hbm, ...), custom_call_target="tpu_custom_call" | custom-call | tf_op jit(solution)/shard_map/combine/pallas_call | solution.py:407
Async XLA Ops:
  7.2 182.1 %reduce-scatter.2.cloned.1.call-start = ((), (), s32[]{:S(2)}) async-start(), calls=%async_computation.4 | async-start | bytes 9469952 | tf_op jit(solution)/shard_map/reduce_scatter | solution.py:398
  7.2 75.3 %copy-start.3 = (bf16[1,512,2048]{2,1,0:T(8,128)(2,1)S(1)}, bf16[1,512,2048]{2,1,0:T(8,128)(2,1)}, u32[]{:S(2)}) copy-start(bf16[1,512,2048]{2,1,0:T(8,128)(2,1)} %param.13) | copy-start | bytes 6291460
  10.3 72.3 %copy-start.1 = (bf16[1,2048,512]{2,1,0:T(8,128)(2,1)S(1)}, bf16[1,2048,512]{2,1,0:T(8,128)(2,1)}, u32[]{:S(2)}) copy-start(bf16[1,2048,512]{2,1,0:T(8,128)(2,1)} %param.11) | copy-start | bytes 6291460
  10.3 72.3 %copy-start.2 = (bf16[1,2048,512]{2,1,0:T(8,128)(2,1)S(1)}, bf16[1,2048,512]{2,1,0:T(8,128)(2,1)}, u32[]{:S(2)}) copy-start(bf16[1,2048,512]{2,1,0:T(8,128)(2,1)} %param.12) | copy-start | bytes 6291460
  172.3 5.0 %copy-start = (bf16[16,1536,128]{2,1,0:T(8,128)(2,1)}, bf16[16,1536,128]{2,1,0:T(8,128)(2,1)S(1)}, u32[]{:S(2)}) copy-start(bf16[16,1536,128]{2,1,0:T(8,128)(2,1)S(1)} %all_to_all.16.arrived_ref.arrived_hbm) | copy-start | bytes 18874372
  172.3 17.0 %copy-start.4 = (bf16[128,2]{0,1:T(2,128)(2,1)S(1)}, bf16[128,2]{0,1:T(2,128)(2,1)}, u32[]{:S(2)}) copy-start(bf16[128,2]{0,1:T(2,128)(2,1)} %param.9) | copy-start | bytes 1540
Sparse Core Ops, SparseCore 0:
  93.7 69.5 reduce-scatter.1

commit v4 on v3

--- a/solution.py
+++ b/solution.py
@@ -236,13 +236,18 @@
     member = flag((iota((rows, lanes), 0) >> 4) == iota((rows, lanes), 1))
     fold = flag((iota((replicas, rows), 1) >> 4) == iota((replicas, rows), 0))
     result = jnp.zeros((replicas, lanes), F32)
+    totals = [jnp.zeros(square, F32) for _ in range(kinds)]
+    size = hidden_width // 4
+    for part in range(0, hidden_width, size):
+        for m in range(kinds):
+            base = m * hidden_width + part
+            pieces = jnp.concatenate(
+                [arrived_ref[:, at : at + group, :].reshape(rows, lanes) for at in range(base, base + size, group)],
+                axis=1,
+            )
+            totals[m] = totals[m] + matmul(pieces, pieces, 1, 1)
     for m in range(kinds):
-        pieces = [
-            arrived_ref[:, at : at + group, :].reshape(rows, lanes)
-            for at in range(m * hidden_width, (m + 1) * hidden_width, group)
-        ]
-        pieces = jnp.concatenate(pieces, axis=1)
-        total = matmul(pieces, pieces, 1, 1)
+        total = totals[m]
         folded = matmul(total * same, member, precision=lax.Precision.HIGHEST)
         gram = matmul(fold, folded, precision=lax.Precision.HIGHEST)
         result = result + (pltpu.roll(gram, m * replicas, 1) if m else gram)
@@ -250,20 +255,29 @@
         out_ref[j] = result
 
 
-def combine_kernel(
-    replicas, partial_ref, arrived_hbm, back_hbm, probs_ref, gate_ref, up_ref, down_ref, grad_hbm, router_ref,
-    arrived_ref, back_ref, arrived_sem, back_sem, grad_sem,
-):
-    tokens = grad_hbm.shape[0]
-    third = arrived_hbm.shape[1] // 3
-    loads = []
-    for m in range(3):
-        piece = (slice(None), slice(m * third, (m + 1) * third))
-        loads.append(pltpu.make_async_copy(arrived_hbm.at[piece], arrived_ref.at[piece], arrived_sem.at[m]))
+def finish_kernel(back_hbm, probs_ref, grad_hbm, router_ref, back_ref, load_sem, store_sem):
+    tokens, width = grad_hbm.shape
+    parts = store_sem.shape[0]
+    size = tokens // parts
+    loads = [pltpu.make_async_copy(back_hbm.at[tokens:, :], back_ref.at[tokens:, :], load_sem.at[parts])]
+    stores = []
+    for part in range(parts):
+        rows = slice(part * size, (part + 1) * size)
+        loads.append(pltpu.make_async_copy(back_hbm.at[rows, :], back_ref.at[rows, :], load_sem.at[part]))
+        stores.append(pltpu.make_async_copy(back_ref.at[rows, :], grad_hbm.at[rows, :], store_sem.at[part]))
     for load in loads:
         load.start()
-    back_copy = pltpu.make_async_copy(back_hbm, back_ref, back_sem)
-    back_copy.start()
+    loads[0].wait()
+    dots = back_ref[tokens:, 0:tokens].astype(F32)
+    router_ref[...] = ((dots[0:2, :] + dots[2:4, :]) / probs_ref[...].astype(F32)).astype(BF16)
+    for load, store in zip(loads[1:], stores):
+        load.wait()
+        store.start()
+    for store in stores:
+        store.wait()
+
+
+def combine_kernel(replicas, partial_ref, arrived_ref, gate_ref, up_ref, down_ref):
     kinds = 3
     lanes = partial_ref.shape[2]
     hidden_width = arrived_ref.shape[1] // kinds
@@ -308,11 +322,6 @@
         scalars = [
             jnp.sum(weights * flag(lane == d), axis=(0, 1), keepdims=True) for d in range(replicas)
         ]
-        loads[m].wait()
-        if m == 2:
-            back_copy.wait()
-            grad_copy = pltpu.make_async_copy(back_ref.at[0:tokens, :], grad_hbm, grad_sem)
-            grad_copy.start()
         step = 128
         for at in range(0, hidden_width, step):
             start = m * hidden_width + at
@@ -323,9 +332,6 @@
                 down_ref[at : at + step, :] = total
             else:
                 (gate_ref, up_ref)[m][:, at : at + step] = total.T
-    dots = back_ref[tokens : tokens + 8, 0:tokens].astype(F32)
-    router_ref[...] = ((dots[0:2, :] + dots[2:4, :]) / probs_ref[...].astype(F32)).astype(BF16)
-    grad_copy.wait()
 
 
 def call(kernel, name, out_shapes, mib, scratch=(), specs=None, out_specs=None):
@@ -401,30 +407,29 @@
     arrived = lax.all_to_all(blocks, "dp", 0, 0, tiled=True)
     partial = call(
         functools.partial(gram_kernel, replicas),
-        "gram", shape((replicas, replicas, 128), F32), 20,
+        "gram", shape((replicas, replicas, 128), F32), 12,
     )(arrived)
     partials = lax.all_to_all(partial, "dp", 0, 0, tiled=True)
-    grad_gate, grad_up, grad_down, input_grad, router_grad = call(
+    grad_gate, grad_up, grad_down = call(
         functools.partial(combine_kernel, replicas),
         "combine",
         (
             shape((shard, hidden_width), F32),
             shape((shard, hidden_width), F32),
             shape((hidden_width, shard), F32),
-            pltpu.HBM((rows_here, width), BF16),
-            shape((top_count, rows_here), BF16),
         ),
-        16,
-        (
-            pltpu.VMEM((replicas, 3 * hidden_width, shard), BF16),
-            pltpu.VMEM((rows_here + 8, width), BF16),
-            dma((3,)),
-            dma,
-            dma,
-        ),
-        specs=[VMEM, in_hbm, in_hbm, VMEM],
-        out_specs=(VMEM, VMEM, VMEM, in_hbm, VMEM),
-    )(partials, pinned(arrived), pinned(back), prob_rows)
+        12,
+    )(partials, arrived)
+    grad_gate, back = lax.optimization_barrier((grad_gate, back))
+    input_grad, router_grad = call(
+        finish_kernel,
+        "finish",
+        (pltpu.HBM((rows_here, width), BF16), shape((top_count, rows_here), BF16)),
+        4,
+        (pltpu.VMEM((rows_here + 8, width), BF16), dma((5,)), dma((4,))),
+        specs=[in_hbm, VMEM],
+        out_specs=(in_hbm, VMEM),
+    )(pinned(back), prob_rows)
     return (grad_gate[None], grad_up[None], grad_down[None], input_grad, router_grad.T)
 
 

time: 202 us -> 201 us (level)
    pallas_call x1, Pallas kernels: 5.46 us -> 2.89 us  [per_device(): call(functools.partial(combine_kernel, replicas), 'combine', (shape((shar...]
    pallas_call x0 -> x1, Pallas kernels: none -> 2.35 us  [per_device(): call(finish_kernel, 'finish', (pltpu.HBM((rows_here, width), BF16), shape...]
  transfers between devices with their start and end apart: 1 -> 1, of which waited for: 0 -> 0; matrix products, arithmetic and copies ran while one was open for 0% -> 0% of each run, Pallas kernels for 2% -> 3%
where the time goes in v4:
time: 201 us; the launch traced here: 200 us
  blocking collectives  163 us (81%)
  Pallas kernels  23.2 us (12%)
  between operations  14.1 us (7%)
    all_to_all x1, blocking collectives, per_device(): arrived = lax.all_to_all(blocks, 'dp', 0, 0, tiled=True)  78.8 us
    all_to_all x1, blocking collectives, per_device(): mixed = lax.all_to_all(send, 'expert', 0, 0, tiled=True)  72.3 us
    all_to_all x1, blocking collectives, per_device(): partials = lax.all_to_all(partial, 'dp', 0, 0, tiled=True)  11.9 us
    pallas_call x1, Pallas kernels, per_device(): call(functools.partial(expert_kernel, capacity), 'expert', (pltpu.HBM((re...  10.9 us
  transfers between devices with their start and end apart: 1, of which 0 were waited for; matrix products, arithmetic and copies ran while one was open for 0% of the time, Pallas kernels for 3%

profile of v4, /device:TPU:2, one launch (start us, length us, event | category | flops | bytes accessed | tf_op | source)
XLA Modules:
  0.0 200.4 jit_solution(882341300574816205)
XLA Ops:
  7.2 0.0 reduce-scatter.2.cloned.1.call-start
  7.2 0.0 copy-start.2
  7.2 3.0 %dispatch.1 = bf16[16,648,128]{2,1,0:T(8,128)(2,1)S(1)} custom-call(s32[2,128]{1,0:T(2,128)} %bitcast.16, bf16[2,128]{1,0:T(2,128)(2,1)} %bitcast.13, bf16[128,2048]{1,0:T(8,128)(2,1)} %tokens_hbm.1, bf16[128,2048]{1,0:T(8,128)(2,1)} %cot_hbm.1), custom_call_target="tpu_custom_call" | custom-call | tf_op jit(solution)/shard_map/dispatch/pallas_call | solution.py:371
  10.3 0.0 copy-start
  10.3 0.0 copy-start.1
  10.3 72.3 %all_to_all.15.mixed_ref = bf16[16,648,128]{2,1,0:T(8,128)(2,1)S(1)} all-to-all(bf16[16,648,128]{2,1,0:T(8,128)(2,1)S(1)} %dispatch.1), channel_id=1, replica_groups=mesh['dp'=16,'expert'=16] {'expert'}, dimensions={0} | all-to-all | bytes 5308416 | tf_op jit(solution)/shard_map/all_to_all | solution.py:383
  82.6 0.0 copy-done.2
  82.6 0.0 copy-done
  82.6 0.0 copy-done.1
  82.6 10.9 %expert.1 = (bf16[16,1536,128]{2,1,0:T(8,128)(2,1)}, bf16[16,136,2048]{2,1,0:T(8,128)(2,1)}) custom-call(bf16[16,648,128]{2,1,0:T(8,128)(2,1)S(1)} %all_to_all.15.mixed_ref, bf16[2048,512]{1,0:T(8,128)(2,1)S(1)} %bitcast.10, bf16[2048,512]{1,0:T(8,128)(2,1)S(1)} %bitcast.11, bf16[512,2048]{1,0:T(8,128)(2,1)S(1)} %bitcast.12), custom_call_target="tpu_custom_call" | custom-call | tf_op jit(solution)/shard_map/expert/pallas_call | solution.py:384
  93.5 0.0 reduce-scatter.2.cloned.1.call-update
  93.6 78.8 %all_to_all.16.arrived_ref = bf16[16,1536,128]{2,1,0:T(8,128)(2,1)S(1)} all-to-all(bf16[16,1536,128]{2,1,0:T(8,128)(2,1)} %get-tuple-element.14), channel_id=1, replica_groups=mesh['dp'=16,'expert'=16] {'dp'}, dimensions={0} | all-to-all | bytes 12582912 | tf_op jit(solution)/shard_map/all_to_all | solution.py:407
  172.3 4.0 %gram.1 = f32[16,16,128]{2,1,0:T(8,128)S(1)} custom-call(bf16[16,1536,128]{2,1,0:T(8,128)(2,1)S(1)} %all_to_all.16.arrived_ref), custom_call_target="tpu_custom_call" | custom-call | tf_op jit(solution)/shard_map/gram/pallas_call | solution.py:408
  176.3 11.9 %all_to_all.17.partial_ref = f32[16,16,128]{2,1,0:T(8,128)S(1)} all-to-all(f32[16,16,128]{2,1,0:T(8,128)S(1)} %gram.1), channel_id=1, replica_groups=mesh['dp'=16,'expert'=16] {'dp'}, dimensions={0} | all-to-all | bytes 262144 | tf_op jit(solution)/shard_map/all_to_all | solution.py:412
  188.2 0.0 copy-start.3
  188.2 2.9 %combine.1 = (f32[128,512]{1,0:T(8,128)}, f32[128,512]{1,0:T(8,128)}, f32[512,128]{1,0:T(8,128)}) custom-call(f32[16,16,128]{2,1,0:T(8,128)S(1)} %all_to_all.17.partial_ref, bf16[16,1536,128]{2,1,0:T(8,128)(2,1)S(1)} %all_to_all.16.arrived_ref), custom_call_target="tpu_custom_call" | custom-call | tf_op jit(solution)/shard_map/combine/pallas_call | solution.py:413
  191.1 0.0 reduce-scatter.2.cloned.1.call-done.back_hbm
  191.1 0.0 copy-done.3
  191.1 2.4 %finish.1 = (bf16[128,2048]{1,0:T(8,128)(2,1)}, bf16[2,128]{1,0:T(2,128)(2,1)}) custom-call(bf16[136,2048]{1,0:T(8,128)(2,1)} %reduce-scatter.2.cloned.1.call-done.back_hbm, bf16[2,128]{1,0:T(2,128)(2,1)S(1)} %bitcast.14), custom_call_target="tpu_custom_call" | custom-call | tf_op jit(solution)/shard_map/finish/pallas_call | solution.py:424
Async XLA Ops:
  7.2 184.0 %reduce-scatter.2.cloned.1.call-start = ((), (), s32[]{:S(2)}) async-start(), calls=%async_computation.4 | async-start | bytes 9469952 | tf_op jit(solution)/shard_map/reduce_scatter | solution.py:404
  7.2 75.4 %copy-start.2 = (bf16[1,512,2048]{2,1,0:T(8,128)(2,1)S(1)}, bf16[1,512,2048]{2,1,0:T(8,128)(2,1)}, u32[]{:S(2)}) copy-start(bf16[1,512,2048]{2,1,0:T(8,128)(2,1)} %param.13) | copy-start | bytes 6291460
  10.3 72.3 %copy-start = (bf16[1,2048,512]{2,1,0:T(8,128)(2,1)S(1)}, bf16[1,2048,512]{2,1,0:T(8,128)(2,1)}, u32[]{:S(2)}) copy-start(bf16[1,2048,512]{2,1,0:T(8,128)(2,1)} %param.11) | copy-start | bytes 6291460
  10.3 72.3 %copy-start.1 = (bf16[1,2048,512]{2,1,0:T(8,128)(2,1)S(1)}, bf16[1,2048,512]{2,1,0:T(8,128)(2,1)}, u32[]{:S(2)}) copy-start(bf16[1,2048,512]{2,1,0:T(8,128)(2,1)} %param.12) | copy-start | bytes 6291460
  188.2 2.9 %copy-start.3 = (bf16[128,2]{0,1:T(2,128)(2,1)S(1)}, bf16[128,2]{0,1:T(2,128)(2,1)}, u32[]{:S(2)}) copy-start(bf16[128,2]{0,1:T(2,128)(2,1)} %param.9) | copy-start | bytes 1540
Sparse Core Ops, SparseCore 0:
  93.7 69.5 reduce-scatter.1

commit v5 on v4

--- a/solution.py
+++ b/solution.py
@@ -54,7 +54,7 @@
     routing_ref, probs_ref, both_ref, small_sem, wide_sem,
 ):
     tokens, width = tokens_hbm.shape
-    step = 512
+    step = 1024
     routing_copy = pltpu.make_async_copy(routing_hbm, routing_ref, small_sem.at[0])
     probs_copy = pltpu.make_async_copy(probs_hbm, probs_ref, small_sem.at[1])
     routing_copy.start()
@@ -234,7 +234,6 @@
     square = (rows, rows)
     same = flag((iota(square, 0) & (group - 1)) == (iota(square, 1) & (group - 1)))
     member = flag((iota((rows, lanes), 0) >> 4) == iota((rows, lanes), 1))
-    fold = flag((iota((replicas, rows), 1) >> 4) == iota((replicas, rows), 0))
     result = jnp.zeros((replicas, lanes), F32)
     totals = [jnp.zeros(square, F32) for _ in range(kinds)]
     size = hidden_width // 4
@@ -248,8 +247,8 @@
             totals[m] = totals[m] + matmul(pieces, pieces, 1, 1)
     for m in range(kinds):
         total = totals[m]
-        folded = matmul(total * same, member, precision=lax.Precision.HIGHEST)
-        gram = matmul(fold, folded, precision=lax.Precision.HIGHEST)
+        folded = jnp.sum((total * same).reshape(replicas, group, rows), axis=1)
+        gram = matmul(folded, member, precision=lax.Precision.HIGHEST)
         result = result + (pltpu.roll(gram, m * replicas, 1) if m else gram)
     for j in range(out_ref.shape[0]):
         out_ref[j] = result

time: 201 us -> 198 us (0.985)
  Pallas kernels: 23.2 us -> 21 us
where the time goes in v5:
time: 198 us
  blocking collectives  163 us (82%)
  Pallas kernels  21 us (11%)
  between operations  14.1 us (7%)
    all_to_all x1, blocking collectives, per_device(): arrived = lax.all_to_all(blocks, 'dp', 0, 0, tiled=True)  78.8 us
    all_to_all x1, blocking collectives, per_device(): mixed = lax.all_to_all(send, 'expert', 0, 0, tiled=True)  72.3 us
    all_to_all x1, blocking collectives, per_device(): partials = lax.all_to_all(partial, 'dp', 0, 0, tiled=True)  11.9 us
    pallas_call x1, Pallas kernels, per_device(): call(functools.partial(expert_kernel, capacity), 'expert', (pltpu.HBM((re...  11 us
  transfers between devices with their start and end apart: 1, of which 0 were waited for; matrix products, arithmetic and copies ran while one was open for 0% of the time, Pallas kernels for 3%

profile of v5, /device:TPU:2, one launch (start us, length us, event | category | flops | bytes accessed | tf_op | source)
XLA Modules:
  0.0 198.2 jit_solution(2657511867181606776)
XLA Ops:
  7.2 0.0 reduce-scatter.2.cloned.1.call-start
  7.2 0.0 copy-start.2
  7.2 2.6 %dispatch.1 = bf16[16,648,128]{2,1,0:T(8,128)(2,1)S(1)} custom-call(s32[2,128]{1,0:T(2,128)} %bitcast.16, bf16[2,128]{1,0:T(2,128)(2,1)} %bitcast.13, bf16[128,2048]{1,0:T(8,128)(2,1)} %tokens_hbm.1, bf16[128,2048]{1,0:T(8,128)(2,1)} %cot_hbm.1), custom_call_target="tpu_custom_call" | custom-call | tf_op jit(solution)/shard_map/dispatch/pallas_call | solution.py:370
  9.8 0.0 copy-start
  9.8 0.0 copy-start.1
  9.8 72.3 %all_to_all.15.mixed_ref = bf16[16,648,128]{2,1,0:T(8,128)(2,1)S(1)} all-to-all(bf16[16,648,128]{2,1,0:T(8,128)(2,1)S(1)} %dispatch.1), channel_id=1, replica_groups=mesh['dp'=16,'expert'=16] {'expert'}, dimensions={0} | all-to-all | bytes 5308416 | tf_op jit(solution)/shard_map/all_to_all | solution.py:382
  82.1 0.0 copy-done.2
  82.1 0.0 copy-done
  82.1 0.0 copy-done.1
  82.1 11.0 %expert.1 = (bf16[16,1536,128]{2,1,0:T(8,128)(2,1)}, bf16[16,136,2048]{2,1,0:T(8,128)(2,1)}) custom-call(bf16[16,648,128]{2,1,0:T(8,128)(2,1)S(1)} %all_to_all.15.mixed_ref, bf16[2048,512]{1,0:T(8,128)(2,1)S(1)} %bitcast.10, bf16[2048,512]{1,0:T(8,128)(2,1)S(1)} %bitcast.11, bf16[512,2048]{1,0:T(8,128)(2,1)S(1)} %bitcast.12), custom_call_target="tpu_custom_call" | custom-call | tf_op jit(solution)/shard_map/expert/pallas_call | solution.py:383
  93.1 0.0 reduce-scatter.2.cloned.1.call-update
  93.1 78.8 %all_to_all.16.arrived_ref = bf16[16,1536,128]{2,1,0:T(8,128)(2,1)S(1)} all-to-all(bf16[16,1536,128]{2,1,0:T(8,128)(2,1)} %get-tuple-element.14), channel_id=1, replica_groups=mesh['dp'=16,'expert'=16] {'dp'}, dimensions={0} | all-to-all | bytes 12582912 | tf_op jit(solution)/shard_map/all_to_all | solution.py:406
  171.9 2.2 %gram.1 = f32[16,16,128]{2,1,0:T(8,128)S(1)} custom-call(bf16[16,1536,128]{2,1,0:T(8,128)(2,1)S(1)} %all_to_all.16.arrived_ref), custom_call_target="tpu_custom_call" | custom-call | tf_op jit(solution)/shard_map/gram/pallas_call | solution.py:407
  174.1 11.9 %all_to_all.17.partial_ref = f32[16,16,128]{2,1,0:T(8,128)S(1)} all-to-all(f32[16,16,128]{2,1,0:T(8,128)S(1)} %gram.1), channel_id=1, replica_groups=mesh['dp'=16,'expert'=16] {'dp'}, dimensions={0} | all-to-all | bytes 262144 | tf_op jit(solution)/shard_map/all_to_all | solution.py:411
  186.0 0.0 copy-start.3
  186.0 2.9 %combine.1 = (f32[128,512]{1,0:T(8,128)}, f32[128,512]{1,0:T(8,128)}, f32[512,128]{1,0:T(8,128)}) custom-call(f32[16,16,128]{2,1,0:T(8,128)S(1)} %all_to_all.17.partial_ref, bf16[16,1536,128]{2,1,0:T(8,128)(2,1)S(1)} %all_to_all.16.arrived_ref), custom_call_target="tpu_custom_call" | custom-call | tf_op jit(solution)/shard_map/combine/pallas_call | solution.py:412
  188.9 0.0 reduce-scatter.2.cloned.1.call-done.back_hbm
  188.9 0.0 copy-done.3
  188.9 2.4 %finish.1 = (bf16[128,2048]{1,0:T(8,128)(2,1)}, bf16[2,128]{1,0:T(2,128)(2,1)}) custom-call(bf16[136,2048]{1,0:T(8,128)(2,1)} %reduce-scatter.2.cloned.1.call-done.back_hbm, bf16[2,128]{1,0:T(2,128)(2,1)S(1)} %bitcast.14), custom_call_target="tpu_custom_call" | custom-call | tf_op jit(solution)/shard_map/finish/pallas_call | solution.py:423
Async XLA Ops:
  7.2 181.8 %reduce-scatter.2.cloned.1.call-start = ((), (), s32[]{:S(2)}) async-start(), calls=%async_computation.4 | async-start | bytes 9469952 | tf_op jit(solution)/shard_map/reduce_scatter | solution.py:403
  7.2 74.9 %copy-start.2 = (bf16[1,512,2048]{2,1,0:T(8,128)(2,1)S(1)}, bf16[1,512,2048]{2,1,0:T(8,128)(2,1)}, u32[]{:S(2)}) copy-start(bf16[1,512,2048]{2,1,0:T(8,128)(2,1)} %param.13) | copy-start | bytes 6291460
  9.8 72.3 %copy-start = (bf16[1,2048,512]{2,1,0:T(8,128)(2,1)S(1)}, bf16[1,2048,512]{2,1,0:T(8,128)(2,1)}, u32[]{:S(2)}) copy-start(bf16[1,2048,512]{2,1,0:T(8,128)(2,1)} %param.11) | copy-start | bytes 6291460
  9.8 72.3 %copy-start.1 = (bf16[1,2048,512]{2,1,0:T(8,128)(2,1)S(1)}, bf16[1,2048,512]{2,1,0:T(8,128)(2,1)}, u32[]{:S(2)}) copy-start(bf16[1,2048,512]{2,1,0:T(8,128)(2,1)} %param.12) | copy-start | bytes 6291460
  186.0 2.9 %copy-start.3 = (bf16[128,2]{0,1:T(2,128)(2,1)S(1)}, bf16[128,2]{0,1:T(2,128)(2,1)}, u32[]{:S(2)}) copy-start(bf16[128,2]{0,1:T(2,128)(2,1)} %param.9) | copy-start | bytes 1540
Sparse Core Ops, SparseCore 0:
  93.2 69.4 reduce-scatter.1

commit v6 on v5

--- a/solution.py
+++ b/solution.py
@@ -128,22 +128,6 @@
             routed_ref[into, columns] = mixed_ref[e, c * pair : c * pair + capacity, :]
             scaled_ref[into, columns] = mixed_ref[e, c * pair + capacity : (c + 1) * pair, :]
     step = 512
-    routed = routed_ref[...]
-    scaled = scaled_ref[...]
-    gate_pre = matmul(routed, gate_ref[...])
-    up_pre = matmul(routed, up_ref[...])
-    hidden_grad = matmul(scaled, down_ref[...], 1, 1)
-    sigmoid = 1.0 / (1.0 + jnp.exp(-gate_pre))
-    activated = gate_pre * sigmoid
-    hidden = (activated * up_pre).astype(BF16)
-    up_grad = (hidden_grad * activated).astype(BF16)
-    gate_grad = (hidden_grad * up_pre * sigmoid * (1.0 + gate_pre * (1.0 - sigmoid))).astype(BF16)
-    dots = jnp.sum(hidden.astype(F32) * hidden_grad, axis=1, keepdims=True)
-    for at in range(0, width, step):
-        rows_grad_ref[:, at : at + step] = (
-            matmul(gate_grad, gate_ref[at : at + step, :], 1, 1)
-            + matmul(up_grad, up_ref[at : at + step, :], 1, 1)
-        ).astype(BF16)
     notes_at = width // lanes * pair
     notes = mixed_ref[:, notes_at : notes_at + 8, :].astype(F32).reshape(8 * blocks, lanes).astype(BF16)
     slot = iota((slots, lanes), 0)
@@ -162,6 +146,22 @@
     taken = flag(iota((slots, tokens), 1).astype(F32) + 1.0 == named)
     first = taken * leading
     second = taken - first
+    routed = routed_ref[...]
+    scaled = scaled_ref[...]
+    gate_pre = matmul(routed, gate_ref[...])
+    up_pre = matmul(routed, up_ref[...])
+    hidden_grad = matmul(scaled, down_ref[...], 1, 1)
+    sigmoid = 1.0 / (1.0 + jnp.exp(-gate_pre))
+    activated = gate_pre * sigmoid
+    hidden = (activated * up_pre).astype(BF16)
+    up_grad = (hidden_grad * activated).astype(BF16)
+    gate_grad = (hidden_grad * up_pre * sigmoid * (1.0 + gate_pre * (1.0 - sigmoid))).astype(BF16)
+    dots = jnp.sum(hidden.astype(F32) * hidden_grad, axis=1, keepdims=True)
+    for at in range(0, width, step):
+        rows_grad_ref[:, at : at + step] = (
+            matmul(gate_grad, gate_ref[at : at + step, :], 1, 1)
+            + matmul(up_grad, up_ref[at : at + step, :], 1, 1)
+        ).astype(BF16)
     high = dots.astype(BF16).astype(F32)
     low = (dots - high).astype(BF16).astype(F32)
     extra_row = iota((8 * blocks, slots), 0)
@@ -206,7 +206,7 @@
         copies.append(copy)
     shard = blocks_ref.shape[2]
     scaling = 1.0 / slots
-    step = 4 * shard
+    step = 8 * shard
     both_t = jnp.concatenate([gate_grad.T, up_grad.T], axis=0)
     made = []
     for left, right_ref, row in ((both_t, routed_ref, 0), (hidden.T, scaled_ref, 2 * hidden_width)):
@@ -287,6 +287,7 @@
     lane = iota((replicas, lanes), 1)
     diagonal = flag(row == lane)
     inside = flag(lane < replicas)
+    all_scalars = []
     for m in range(kinds):
         gram = (pltpu.roll(summed, lanes - m * replicas, 1) if m else summed) * inside
         weights = diagonal
@@ -318,9 +319,10 @@
                 former_col * weights + latter_col * pltpu.roll(weights, replicas - half, 0)
             )
             half //= 2
-        scalars = [
-            jnp.sum(weights * flag(lane == d), axis=(0, 1), keepdims=True) for d in range(replicas)
-        ]
+        all_scalars.append(
+            [jnp.sum(weights * flag(lane == d), axis=(0, 1), keepdims=True) for d in range(replicas)]
+        )
+    for m, scalars in enumerate(all_scalars):
         step = 128
         for at in range(0, hidden_width, step):
             start = m * hidden_width + at

time: 198 us -> 198 us (level)
  no operation moved by 1% of the time
where the time goes in v6:
time: 198 us
  blocking collectives  163 us (82%)
  Pallas kernels  20.6 us (10%)
  between operations  14.1 us (7%)
    all_to_all x1, blocking collectives, per_device(): arrived = lax.all_to_all(blocks, 'dp', 0, 0, tiled=True)  78.8 us
    all_to_all x1, blocking collectives, per_device(): mixed = lax.all_to_all(send, 'expert', 0, 0, tiled=True)  72.3 us
    all_to_all x1, blocking collectives, per_device(): partials = lax.all_to_all(partial, 'dp', 0, 0, tiled=True)  11.9 us
    pallas_call x1, Pallas kernels, per_device(): call(functools.partial(expert_kernel, capacity), 'expert', (pltpu.HBM((re...  10.5 us
  transfers between devices with their start and end apart: 1, of which 0 were waited for; matrix products, arithmetic and copies ran while one was open for 0% of the time, Pallas kernels for 3%

profile of v6, /device:TPU:2, one launch (start us, length us, event | category | flops | bytes accessed | tf_op | source)
XLA Modules:
  0.0 197.7 jit_solution(2359926411734336557)
XLA Ops:
  7.2 0.0 reduce-scatter.2.cloned.1.call-start
  7.2 0.0 copy-start.2
  7.2 2.6 %dispatch.1 = bf16[16,648,128]{2,1,0:T(8,128)(2,1)S(1)} custom-call(s32[2,128]{1,0:T(2,128)} %bitcast.16, bf16[2,128]{1,0:T(2,128)(2,1)} %bitcast.13, bf16[128,2048]{1,0:T(8,128)(2,1)} %tokens_hbm.1, bf16[128,2048]{1,0:T(8,128)(2,1)} %cot_hbm.1), custom_call_target="tpu_custom_call" | custom-call | tf_op jit(solution)/shard_map/dispatch/pallas_call | solution.py:372
  9.8 0.0 copy-start
  9.8 0.0 copy-start.1
  9.8 72.3 %all_to_all.15.mixed_ref = bf16[16,648,128]{2,1,0:T(8,128)(2,1)S(1)} all-to-all(bf16[16,648,128]{2,1,0:T(8,128)(2,1)S(1)} %dispatch.1), channel_id=1, replica_groups=mesh['dp'=16,'expert'=16] {'expert'}, dimensions={0} | all-to-all | bytes 5308416 | tf_op jit(solution)/shard_map/all_to_all | solution.py:384
  82.1 0.0 copy-done.2
  82.1 0.0 copy-done
  82.1 0.0 copy-done.1
  82.1 10.5 %expert.1 = (bf16[16,1536,128]{2,1,0:T(8,128)(2,1)}, bf16[16,136,2048]{2,1,0:T(8,128)(2,1)}) custom-call(bf16[16,648,128]{2,1,0:T(8,128)(2,1)S(1)} %all_to_all.15.mixed_ref, bf16[2048,512]{1,0:T(8,128)(2,1)S(1)} %bitcast.10, bf16[2048,512]{1,0:T(8,128)(2,1)S(1)} %bitcast.11, bf16[512,2048]{1,0:T(8,128)(2,1)S(1)} %bitcast.12), custom_call_target="tpu_custom_call" | custom-call | tf_op jit(solution)/shard_map/expert/pallas_call | solution.py:385
  92.6 0.0 reduce-scatter.2.cloned.1.call-update
  92.7 78.8 %all_to_all.16.arrived_ref = bf16[16,1536,128]{2,1,0:T(8,128)(2,1)S(1)} all-to-all(bf16[16,1536,128]{2,1,0:T(8,128)(2,1)} %get-tuple-element.14), channel_id=1, replica_groups=mesh['dp'=16,'expert'=16] {'dp'}, dimensions={0} | all-to-all | bytes 12582912 | tf_op jit(solution)/shard_map/all_to_all | solution.py:408
  171.4 2.2 %gram.1 = f32[16,16,128]{2,1,0:T(8,128)S(1)} custom-call(bf16[16,1536,128]{2,1,0:T(8,128)(2,1)S(1)} %all_to_all.16.arrived_ref), custom_call_target="tpu_custom_call" | custom-call | tf_op jit(solution)/shard_map/gram/pallas_call | solution.py:409
  173.7 11.9 %all_to_all.17.partial_ref = f32[16,16,128]{2,1,0:T(8,128)S(1)} all-to-all(f32[16,16,128]{2,1,0:T(8,128)S(1)} %gram.1), channel_id=1, replica_groups=mesh['dp'=16,'expert'=16] {'dp'}, dimensions={0} | all-to-all | bytes 262144 | tf_op jit(solution)/shard_map/all_to_all | solution.py:413
  185.6 0.0 copy-start.3
  185.6 2.9 %combine.1 = (f32[128,512]{1,0:T(8,128)}, f32[128,512]{1,0:T(8,128)}, f32[512,128]{1,0:T(8,128)}) custom-call(f32[16,16,128]{2,1,0:T(8,128)S(1)} %all_to_all.17.partial_ref, bf16[16,1536,128]{2,1,0:T(8,128)(2,1)S(1)} %all_to_all.16.arrived_ref), custom_call_target="tpu_custom_call" | custom-call | tf_op jit(solution)/shard_map/combine/pallas_call | solution.py:414
  188.5 0.0 reduce-scatter.2.cloned.1.call-done.back_hbm
  188.5 0.0 copy-done.3
  188.5 2.4 %finish.1 = (bf16[128,2048]{1,0:T(8,128)(2,1)}, bf16[2,128]{1,0:T(2,128)(2,1)}) custom-call(bf16[136,2048]{1,0:T(8,128)(2,1)} %reduce-scatter.2.cloned.1.call-done.back_hbm, bf16[2,128]{1,0:T(2,128)(2,1)S(1)} %bitcast.14), custom_call_target="tpu_custom_call" | custom-call | tf_op jit(solution)/shard_map/finish/pallas_call | solution.py:425
Async XLA Ops:
  7.2 181.3 %reduce-scatter.2.cloned.1.call-start = ((), (), s32[]{:S(2)}) async-start(), calls=%async_computation.4 | async-start | bytes 9469952 | tf_op jit(solution)/shard_map/reduce_scatter | solution.py:405
  7.2 74.9 %copy-start.2 = (bf16[1,512,2048]{2,1,0:T(8,128)(2,1)S(1)}, bf16[1,512,2048]{2,1,0:T(8,128)(2,1)}, u32[]{:S(2)}) copy-start(bf16[1,512,2048]{2,1,0:T(8,128)(2,1)} %param.13) | copy-start | bytes 6291460
  9.8 72.3 %copy-start = (bf16[1,2048,512]{2,1,0:T(8,128)(2,1)S(1)}, bf16[1,2048,512]{2,1,0:T(8,128)(2,1)}, u32[]{:S(2)}) copy-start(bf16[1,2048,512]{2,1,0:T(8,128)(2,1)} %param.11) | copy-start | bytes 6291460
  9.8 72.3 %copy-start.1 = (bf16[1,2048,512]{2,1,0:T(8,128)(2,1)S(1)}, bf16[1,2048,512]{2,1,0:T(8,128)(2,1)}, u32[]{:S(2)}) copy-start(bf16[1,2048,512]{2,1,0:T(8,128)(2,1)} %param.12) | copy-start | bytes 6291460
  185.6 2.9 %copy-start.3 = (bf16[128,2]{0,1:T(2,128)(2,1)S(1)}, bf16[128,2]{0,1:T(2,128)(2,1)}, u32[]{:S(2)}) copy-start(bf16[128,2]{0,1:T(2,128)(2,1)} %param.9) | copy-start | bytes 1540
Sparse Core Ops, SparseCore 0:
  92.8 69.3 reduce-scatter.1
